TPU v7x, 32 devices: a whole 2x2x4 slice. The times are simulated.
32 devices in a mesh: dp: 4 (over z), seq: 2 (over x), tensor: 4 (over y, core).
Axes of the slice: x: 2, y: 2, z: 4, core: 2. Of those that a mesh axis runs over, the one named last changes fastest.
Arguments:
- inputs: bfloat16 [4, 4096, 768], P('dp', 'seq'), may hold values from -6 to 6
- pass_embed: float32 [768], replicated, may hold values from -3 to 3
- norm1_gain: float32 [768], replicated, may hold values from 0.5 to 1.5
- norm1_shift: float32 [768], replicated, may hold values from -1 to 1
- w_qkv: bfloat16 [3, 768, 768], P(None, None, 'tensor'), may hold values from -0.21875 to 0.21875
- b_qv: float32 [2, 768], P(None, 'tensor'), may hold values from -1 to 1
- w_out: bfloat16 [768, 768], P('tensor'), may hold values from -0.875 to 0.875
- b_out: float32 [768], replicated, may hold values from -1 to 1
- norm2_gain: float32 [768], replicated, may hold values from 0.5 to 1.5
- norm2_shift: float32 [768], replicated, may hold values from -1 to 1
- w_up: bfloat16 [768, 3072], P(None, 'tensor'), may hold values from -0.21875 to 0.21875
- b_up: float32 [3072], P('tensor'), may hold values from -1.5 to 1.5
- w_down: bfloat16 [3072, 768], P('tensor'), may hold values from -0.109375 to 0.109375
- b_down: float32 [768], replicated, may hold values from -1 to 1
- out_grad: bfloat16 [4, 4096, 768], P('dp', 'seq'), may hold values from -6 to 6
- seg_id: int32 [4, 4096], P('dp'), may hold values from 0 to 12, as said below
- parent: int32 [4, 13], P('dp'), may hold values from 0 to 4, as said below
Outputs:
- output: bfloat16 [4, 4096, 768], P('dp', ('seq', 'tensor'))
- input_grad: bfloat16 [4, 4096, 768], P('dp', ('seq', 'tensor'))
- grad_pass: float32 [768], replicated
- grad_norm1_gain: float32 [768], replicated
- grad_norm1_shift: float32 [768], replicated
- grad_w_qkv: float32 [3, 768, 768], P(None, None, 'tensor')
- grad_b_qv: float32 [2, 768], P(None, 'tensor')
- grad_w_out: float32 [768, 768], P('tensor')
- grad_b_out: float32 [768], replicated
- grad_norm2_gain: float32 [768], replicated
- grad_norm2_shift: float32 [768], replicated
- grad_w_up: float32 [768, 3072], P(None, 'tensor')
- grad_b_up: float32 [3072], P('tensor')
- grad_w_down: float32 [3072, 768], P('tensor')
- grad_b_down: float32 [768], replicated
Inputs may be any that keep to these rules, and one draw needn't show every extreme that they name: `seg_id`: in each tree segment 0 (the trunk) covers 1024 consecutive tokens starting at a multiple of 1024; each other segment covers 256 consecutive tokens starting at a multiple of 256. Segment 0 is its own parent; segments 1 to 4 have parent 0; each of them is the parent of exactly two of the other segments.
All inputs are finite; a program needn't handle non-finite values.
Results may differ from a plain program's by a relative error of at most 0.019.
Values may be sent and summed in bfloat16 or wider, within the bound.
No kernel may reach another device: no remote copies, remote signals or barrier semaphores. Data moves between devices by JAX's collectives and lax.ppermute only.
A program may use at most 256 MiB of HBM per device.

v0:
```python
import jax
import jax.numpy as jnp
from jax import lax
from jax.sharding import PartitionSpec as P

HD = 64


EPS = 1e-05
ROOT = 0.7978845608028654


def norm_stats(values):
    row_mean = jnp.mean(values, -1, keepdims=True)
    centred = values - row_mean
    inv_std = lax.rsqrt(jnp.mean(centred * centred, -1, keepdims=True) + EPS)
    return (centred * inv_std, inv_std)


def norm_back(grad_out, normal, inv_std, gain_vec):
    scaled = grad_out * gain_vec
    return inv_std * (
        scaled
        - jnp.mean(scaled, -1, keepdims=True)
        - normal * jnp.mean(scaled * normal, -1, keepdims=True)
    )


def gelu_parts(pre_act):
    cubic_term = 0.044715 * pre_act * pre_act * pre_act
    tangent = jnp.tanh(ROOT * (pre_act + cubic_term))
    gelu_value = 0.5 * pre_act * (1.0 + tangent)
    gelu_slope = 0.5 * (1.0 + tangent) + 0.5 * pre_act * (1.0 - tangent * tangent) * ROOT * (
        1.0 + 3.0 * 0.044715 * pre_act * pre_act
    )
    return (gelu_value, gelu_slope)


def forward_rows(left, right):
    return jnp.einsum("tbd,de->tbe", left, right, preferred_element_type=jnp.float32)


def weight_grad(left, right):
    return jnp.einsum("tbd,tbe->de", left, right, preferred_element_type=jnp.float32)


def input_rows(grad_rows, weight):
    return jnp.einsum("tbe,de->tbd", grad_rows, weight, preferred_element_type=jnp.float32)


def row_total(values):
    return jnp.sum(values.astype(jnp.float32), axis=(0, 1))


def ancestry(parent_row):
    labels = jnp.arange(parent_row.shape[0], dtype=jnp.int32)
    step_up = (
        (parent_row[:, None] == labels[None, :]) & (labels[:, None] != labels[None, :])
    ).astype(jnp.float32)
    return step_up + jnp.dot(step_up, step_up)


def visibility(seg_query, pos_query, seg_keys, ancestor):
    labels = jnp.arange(ancestor.shape[0], dtype=jnp.int32)
    query_hot = (seg_query[:, None] == labels[None, :]).astype(jnp.float32)
    key_hot = (labels[:, None] == seg_keys[None, :]).astype(jnp.float32)
    reachable = jnp.dot(jnp.dot(query_hot, ancestor), key_hot)
    key_pos = jnp.arange(seg_keys.shape[0], dtype=jnp.int32)
    same_seg = (seg_query[:, None] == seg_keys[None, :]) & (pos_query[:, None] >= key_pos[None, :])
    return same_seg | (reachable > 0.5)


def attend(queries, key_heads, value_heads, seg_row, ancestor, first_row):
    block_len = queries.shape[0]
    head_count = key_heads.shape[1]
    blk_width = min(512, block_len)
    blk_count = block_len // blk_width
    q_blocks = queries.reshape(blk_count, blk_width, head_count, HD)
    starts = first_row + blk_width * jnp.arange(blk_count, dtype=jnp.int32)

    def one_block(pieces):
        q_block, blk_start = pieces
        visible = visibility(
            lax.dynamic_slice_in_dim(seg_row, blk_start, blk_width),
            blk_start + jnp.arange(blk_width, dtype=jnp.int32),
            seg_row,
            ancestor,
        )
        scores = (
            jnp.einsum("qhd,khd->hqk", q_block, key_heads, preferred_element_type=jnp.float32)
            * 0.125
        )
        scores = jnp.where(visible[None], scores, -jnp.inf)
        row_top = jnp.max(scores, -1, keepdims=True)
        weights = jnp.exp(scores - row_top)
        row_sum = jnp.sum(weights, -1, keepdims=True)
        prob_low = (weights / row_sum).astype(jnp.bfloat16)
        mixture = jnp.einsum(
            "hqk,khd->qhd", prob_low, value_heads, preferred_element_type=jnp.float32
        )
        return (mixture, (row_top + jnp.log(row_sum))[..., 0])

    mixture, log_sums = lax.map(one_block, (q_blocks, starts))
    return (mixture.reshape(block_len, head_count * HD), log_sums)


def attend_back(queries, key_heads, value_heads, grad_mix, log_sums, seg_row, ancestor, first_row):
    block_len = queries.shape[0]
    head_count = key_heads.shape[1]
    blk_width = min(512, block_len)
    blk_count = block_len // blk_width
    q_blocks = queries.reshape(blk_count, blk_width, head_count, HD)
    g_blocks = grad_mix.reshape(blk_count, blk_width, head_count, HD)
    starts = first_row + blk_width * jnp.arange(blk_count, dtype=jnp.int32)

    def one_block(totals, pieces):
        q_block, g_block, lse_block, blk_start = pieces
        visible = visibility(
            lax.dynamic_slice_in_dim(seg_row, blk_start, blk_width),
            blk_start + jnp.arange(blk_width, dtype=jnp.int32),
            seg_row,
            ancestor,
        )
        scores = (
            jnp.einsum("qhd,khd->hqk", q_block, key_heads, preferred_element_type=jnp.float32)
            * 0.125
        )
        probs_full = jnp.where(visible[None], jnp.exp(scores - lse_block[..., None]), 0.0)
        grad_prob = jnp.einsum(
            "qhd,khd->hqk", g_block, value_heads, preferred_element_type=jnp.float32
        )
        inner = jnp.sum(probs_full * grad_prob, -1, keepdims=True)
        grad_score = (probs_full * (grad_prob - inner)).astype(jnp.bfloat16)
        grad_query = (
            jnp.einsum("hqk,khd->qhd", grad_score, key_heads, preferred_element_type=jnp.float32)
            * 0.125
        )
        key_sum = (
            totals[0]
            + jnp.einsum("hqk,qhd->khd", grad_score, q_block, preferred_element_type=jnp.float32)
            * 0.125
        )
        value_sum = totals[1] + jnp.einsum(
            "hqk,qhd->khd",
            probs_full.astype(jnp.bfloat16),
            g_block,
            preferred_element_type=jnp.float32,
        )
        totals = (key_sum, value_sum)
        return (totals, (grad_query, inner[..., 0]))

    zero_keys = jnp.zeros(key_heads.shape, jnp.float32)
    start_totals = (zero_keys, zero_keys)
    totals, (grad_query, inner) = lax.scan(
        one_block, start_totals, (q_blocks, g_blocks, log_sums, starts)
    )
    length = key_heads.shape[0]
    kv_term = None
    kv_term = jnp.concatenate(
        [totals[0].reshape(length, head_count * HD), totals[1].reshape(length, head_count * HD)], -1
    )
    return (grad_query.reshape(block_len, head_count * HD), inner, kv_term)


def local(
    inputs,
    pass_embed,
    norm1_gain,
    norm1_shift,
    w_qkv,
    b_qv,
    w_out,
    b_out,
    norm2_gain,
    norm2_shift,
    w_up,
    b_up,
    w_down,
    b_down,
    out_grad,
    seg_id,
    parent,
):
    tree_count = inputs.shape[0]
    block_len = inputs.shape[1]
    local_width = w_qkv.shape[2]
    head_count = local_width // HD
    sub_len = block_len // lax.axis_size("tensor")
    sub_start = lax.axis_index("tensor") * sub_len
    first_row = lax.axis_index("seq") * block_len

    def own_rows(values):
        return lax.dynamic_slice_in_dim(values, sub_start, sub_len, 1)

    residual = inputs.astype(jnp.float32) + pass_embed
    norm_one, inv_one = norm_stats(residual)
    normed = (norm_one * norm1_gain + norm1_shift).astype(jnp.bfloat16)
    queries = (forward_rows(normed, w_qkv[0]) + b_qv[0]).astype(jnp.bfloat16)
    key_loc = forward_rows(normed, w_qkv[1]).astype(jnp.bfloat16)
    value_loc = (forward_rows(normed, w_qkv[2]) + b_qv[1]).astype(jnp.bfloat16)
    gathered = lax.all_gather(jnp.concatenate([key_loc, value_loc], -1), "seq", axis=1, tiled=True)
    length = gathered.shape[1]
    key_all = gathered[..., :local_width].reshape(tree_count, length, head_count, HD)
    value_all = gathered[..., local_width:].reshape(tree_count, length, head_count, HD)
    ancestors = [ancestry(parent[0])]
    tree_idx = 0
    mixed_tree, log_sums = attend(
        queries[tree_idx],
        key_all[tree_idx],
        value_all[tree_idx],
        seg_id[tree_idx],
        ancestors[tree_idx],
        first_row,
    )
    mix_list = [mixed_tree]
    lse_list = [log_sums]
    mixture = jnp.stack(mix_list).astype(jnp.bfloat16)
    partial_attn = forward_rows(mixture, w_out)
    middle = (
        residual + lax.psum(partial_attn.astype(jnp.bfloat16), "tensor").astype(jnp.float32) + b_out
    )
    norm_two, inv_two = norm_stats(middle)
    lifted_own = (norm_two * norm2_gain + norm2_shift).astype(jnp.bfloat16)
    pre_act = forward_rows(lifted_own, w_up) + b_up
    gelu_value, gelu_slope = gelu_parts(pre_act)
    active = gelu_value.astype(jnp.bfloat16)
    partial_mlp = forward_rows(active, w_down)
    output = own_rows(
        middle + lax.psum(partial_mlp.astype(jnp.bfloat16), "tensor").astype(jnp.float32) + b_down
    ).astype(jnp.bfloat16)
    grad_w_down = weight_grad(active, out_grad)
    grad_b_down = row_total(out_grad)
    grad_pre = (input_rows(out_grad, w_down) * gelu_slope).astype(jnp.bfloat16)
    grad_w_up = weight_grad(lifted_own, grad_pre)
    grad_b_up = row_total(grad_pre)
    partial_lift = input_rows(grad_pre, w_up)
    grad_lift = lax.psum(partial_lift.astype(jnp.bfloat16), "tensor").astype(jnp.float32)
    grad_middle = out_grad.astype(jnp.float32) + norm_back(grad_lift, norm_two, inv_two, norm2_gain)
    grad_g2 = row_total(grad_lift * norm_two)
    grad_b2 = row_total(grad_lift)
    grad_b_out = row_total(grad_middle)
    proj_low = grad_middle.astype(jnp.bfloat16)
    grad_w_out = weight_grad(mixture, proj_low)
    grad_mix = input_rows(proj_low, w_out).astype(jnp.bfloat16)
    tree_idx = 0
    grad_query, inner, kv_term = attend_back(
        queries[tree_idx],
        key_all[tree_idx],
        value_all[tree_idx],
        grad_mix[tree_idx],
        lse_list[tree_idx],
        seg_id[tree_idx],
        ancestors[tree_idx],
        first_row,
    )
    query_list = [grad_query]
    term_list = [kv_term]
    kv_grads = lax.psum_scatter(
        jnp.stack(term_list).astype(jnp.bfloat16), "seq", scatter_dimension=1, tiled=True
    ).astype(jnp.float32)
    grad_q = jnp.stack(query_list).astype(jnp.bfloat16)
    grad_k = kv_grads[..., :local_width].astype(jnp.bfloat16)
    grad_v = kv_grads[..., local_width:].astype(jnp.bfloat16)
    grad_w_qkv = jnp.stack(
        [weight_grad(normed, grad_q), weight_grad(normed, grad_k), weight_grad(normed, grad_v)]
    )
    grad_b_qv = jnp.stack([row_total(grad_q), row_total(grad_v)])
    partial_norm = (
        input_rows(grad_q, w_qkv[0]) + input_rows(grad_k, w_qkv[1]) + input_rows(grad_v, w_qkv[2])
    )
    grad_norm = lax.psum(partial_norm.astype(jnp.bfloat16), "tensor").astype(jnp.float32)
    grad_resid = grad_middle + norm_back(grad_norm, norm_one, inv_one, norm1_gain)
    input_grad = own_rows(grad_resid).astype(jnp.bfloat16)
    grad_pass = row_total(grad_resid)
    grad_g1 = row_total(grad_norm * norm_one)
    grad_b1 = row_total(grad_norm)
    summed = lax.psum(
        (
            grad_w_qkv,
            grad_b_qv,
            grad_w_out,
            grad_w_up,
            grad_b_up,
            grad_w_down,
            grad_b_down,
            grad_pass,
            grad_g1,
            grad_b1,
            grad_g2,
            grad_b2,
            grad_b_out,
        ),
        ("dp", "seq"),
    )
    return (
        output,
        input_grad,
        summed[7],
        summed[8],
        summed[9],
        summed[0],
        summed[1],
        summed[2],
        summed[12],
        summed[10],
        summed[11],
        summed[3],
        summed[4],
        summed[5],
        summed[6],
    )


def solution(mesh):
    return jax.shard_map(
        local,
        mesh=mesh,
        in_specs=(
            P("dp", "seq", None),
            P(),
            P(),
            P(),
            P(None, None, "tensor"),
            P(None, "tensor"),
            P("tensor", None),
            P(),
            P(),
            P(),
            P(None, "tensor"),
            P("tensor"),
            P("tensor", None),
            P(),
            P("dp", "seq", None),
            P("dp", None),
            P("dp", None),
        ),
        out_specs=(
            P("dp", ("seq", "tensor"), None),
            P("dp", ("seq", "tensor"), None),
            P(),
            P(),
            P(),
            P(None, None, "tensor"),
            P(None, "tensor"),
            P("tensor", None),
            P(),
            P(),
            P(),
            P(None, "tensor"),
            P("tensor"),
            P("tensor", None),
            P(),
        ),
        check_vma=False,
    )
```

profile of v0, /device:TPU:0, one launch (start us, length us, event | category | flops | bytes accessed | tf_op | source)
XLA Modules:
  0.0 1257.6 jit_solution(2198636816615368359)
XLA Ops:
  23.9 43.7 %all-gather.2.cloned.1.call-done = bf16[1,4096,384]{1,2,0:T(8,128)(2,1)} async-done(((bf16[1,2048,384]{1,2,0:T(8,128)(2,1)}), bf16[1,4096,384]{1,2,0:T(8,128)(2,1)}) %all-gather.2.cloned.1.call-update) | async-done | bytes 3145744 | tf_op jit(solution)/shard_map/all_gather | solution.py:201
  71.8 184.0 %while.27 = (s32[]{:T(128)}, bf16[4,512,3,64]{1,3,2,0:T(8,128)(2,1)}, f32[4,3,512]{2,1,0:T(4,128)}, s32[4]{0:T(128)S(1)}, s32[4096]{0:T(1024)}, /*index=5*/s32[1...) while((s32[]{:T(128)}, ...), condition=%wide.region_5.6_spmd, body=%wide.region_2.5_spmd.sunk | while | flops 1751353856 | bytes 108675712 | solution.py:103
  104.9 12.1 fusion.193
  126.8 12.1 fusion.191
  150.9 12.1 fusion.193
  172.8 12.1 fusion.191
  196.9 12.1 fusion.193
  218.7 12.1 fusion.191
  242.8 12.1 fusion.193
  262.8 68.1 %all-reduce.8.cloned.1.call-done = bf16[1,2048,768]{2,1,0:T(8,128)(2,1)} async-done(((bf16[1,2048,768]{2,1,0:T(8,128)(2,1)}), bf16[1,2048,768]{2,1,0:T(8,128)(2,1)}) %all-reduce.8.cloned.1.call-update) | async-done | bytes 3145744 | tf_op jit(solution)/shard_map/psum | solution.py:220
  353.6 68.6 %all-reduce.10.cloned.1.call-done = bf16[1,2048,768]{2,1,0:T(8,128)(2,1)} async-done(((bf16[1,2048,768]{2,1,0:T(8,128)(2,1)}), bf16[1,2048,768]{2,1,0:T(8,128)(2,1)}) %all-reduce.10.cloned.1.call-update) | async-done | bytes 3145744 | tf_op jit(solution)/shard_map/psum | solution.py:237
  444.9 377.5 %while.28 = (s32[]{:T(128)}, f32[4096,3,64]{0,2,1:T(8,128)}, f32[4096,3,64]{0,2,1:T(8,128)}, bf16[4,512,3,64]{1,3,2,0:T(8,128)(2,1)}, bf16[4,512,3,64]{1,3,2,0:T...) while((s32[]{:T(128)}, f32[4096,3,64]{0,2,1:T(8,128)}, ...), condition=%wide.region_15.16_spmd.clone, body=%wide.region_13.15_spmd.clone.sunk | while | flops 4190177792 | bytes 234558224 | solution.py:154
  453.4 13.3 %fusion.205 = f32[3,512,4096]{2,1,0:T(8,128)} fusion(bf16[4096,3,64]{0,2,1:T(8,128)(2,1)} %copy-done.1, bf16[4,512,3,64]{1,3,2,0:T(8,128)(2,1)} %copy-done.15, s32[]{:T(128)S(6)} %copy.60), kind=kOutput, calls=%fused_computation.48.clone.1 | convolution fusion | flops 805306368 | bytes 26935300 | tf_op jit(solution)/shard_map/while/body/eval_jaxpr/qhd,khd->hqk/dot_general | solution.py:125
  466.7 12.5 fusion.208
  479.3 18.3 %multiply_reduce_fusion.4 = (f32[3,512]{1,0:T(4,128)S(1)}, f32[3,512,4096]{2,1,0:T(8,128)}) fusion(f32[3,512,4096]{2,1,0:T(8,128)} %fusion.205, f32[3,512]{1,0:T(4,128)S(1)} %dynamic-slice_bitcast_fusion.2, pred[512,4096]{1,0:T(8,128)(4,1)S(1)} %fusion.206, bf16[4096,3,64]{0,2,1:T(8,128)(2,1)} %get-tuple-element.551, ...), kind=kOutput, calls=%fused_computation.25.clone.1 | convolution fusion | flops 836762112 | bytes 54210564 | tf_op jit(solution)/shard_map/while/body/eval_jaxpr/qhd,khd->hqk/dot_general | solution.py:129
  497.6 21.9 %multiply_convert_fusion.5 = bf16[3,512,4096]{2,1,0:T(8,128)(2,1)} fusion(f32[3,512,4096]{2,1,0:T(8,128)} %get-tuple-element.466, f32[3,512,4096]{2,1,0:T(8,128)} %fusion.205, f32[3,512]{1,0:T(4,128)S(1)} %get-tuple-element.467, f32[3,512]{1,0:T(4,128)S(1)} %dynamic-slice_bitcast_fusion.2, pred[512,4096]{1,0:T(8,128)(4,1)S(1)} %fusion.206), kind=kLoop, calls=%fused_computation.24.clone.1 | loop fusion | flops 37748736 | bytes 65024000 | tf_op jit(solution)/shard_map/while/body/eval_jaxpr/convert_element_type | solution.py:133
  546.2 13.3 %fusion.205 = f32[3,512,4096]{2,1,0:T(8,128)} fusion(bf16[4096,3,64]{0,2,1:T(8,128)(2,1)} %copy-done.1, bf16[4,512,3,64]{1,3,2,0:T(8,128)(2,1)} %copy-done.15, s32[]{:T(128)S(6)} %copy.60), kind=kOutput, calls=%fused_computation.48.clone.1 | convolution fusion | flops 805306368 | bytes 26935300 | tf_op jit(solution)/shard_map/while/body/eval_jaxpr/qhd,khd->hqk/dot_general | solution.py:125
  559.5 13.6 %fusion.208 = f32[4096,3,64]{0,2,1:T(8,128)} fusion(f32[3,512,4096]{2,1,0:T(8,128)} %fusion.205, f32[3,512]{1,0:T(4,128)S(1)} %dynamic-slice_bitcast_fusion.2, pred[512,4096]{1,0:T(8,128)(4,1)S(1)} %fusion.206, f32[4096,3,64]{0,2,1:T(8,128)} %get-tuple-element.525, pred[]{:T(512)S(6)} %compare.3, bf16[4,512,3,64]{1,3,2,0:T(8,128)(2,1)} %get-tuple-element.550, ...), kind=kOutput, calls=%fused_computation.37.clone.1 | convolution fusion | flops 832045056 | bytes 33757188 | tf_op jit(solution)/shard_map/while/body/eval_jaxpr/hqk,qhd->khd/dot_general | solution.py:143
  573.1 18.3 %multiply_reduce_fusion.4 = (f32[3,512]{1,0:T(4,128)S(1)}, f32[3,512,4096]{2,1,0:T(8,128)}) fusion(f32[3,512,4096]{2,1,0:T(8,128)} %fusion.205, f32[3,512]{1,0:T(4,128)S(1)} %dynamic-slice_bitcast_fusion.2, pred[512,4096]{1,0:T(8,128)(4,1)S(1)} %fusion.206, bf16[4096,3,64]{0,2,1:T(8,128)(2,1)} %get-tuple-element.551, ...), kind=kOutput, calls=%fused_computation.25.clone.1 | convolution fusion | flops 836762112 | bytes 54210564 | tf_op jit(solution)/shard_map/while/body/eval_jaxpr/qhd,khd->hqk/dot_general | solution.py:129
  591.4 21.9 %multiply_convert_fusion.5 = bf16[3,512,4096]{2,1,0:T(8,128)(2,1)} fusion(f32[3,512,4096]{2,1,0:T(8,128)} %get-tuple-element.466, f32[3,512,4096]{2,1,0:T(8,128)} %fusion.205, f32[3,512]{1,0:T(4,128)S(1)} %get-tuple-element.467, f32[3,512]{1,0:T(4,128)S(1)} %dynamic-slice_bitcast_fusion.2, pred[512,4096]{1,0:T(8,128)(4,1)S(1)} %fusion.206), kind=kLoop, calls=%fused_computation.24.clone.1 | loop fusion | flops 37748736 | bytes 65024000 | tf_op jit(solution)/shard_map/while/body/eval_jaxpr/convert_element_type | solution.py:133
  640.9 13.3 %fusion.205 = f32[3,512,4096]{2,1,0:T(8,128)} fusion(bf16[4096,3,64]{0,2,1:T(8,128)(2,1)} %copy-done.1, bf16[4,512,3,64]{1,3,2,0:T(8,128)(2,1)} %copy-done.15, s32[]{:T(128)S(6)} %copy.60), kind=kOutput, calls=%fused_computation.48.clone.1 | convolution fusion | flops 805306368 | bytes 26935300 | tf_op jit(solution)/shard_map/while/body/eval_jaxpr/qhd,khd->hqk/dot_general | solution.py:125
  654.2 13.6 %fusion.208 = f32[4096,3,64]{0,2,1:T(8,128)} fusion(f32[3,512,4096]{2,1,0:T(8,128)} %fusion.205, f32[3,512]{1,0:T(4,128)S(1)} %dynamic-slice_bitcast_fusion.2, pred[512,4096]{1,0:T(8,128)(4,1)S(1)} %fusion.206, f32[4096,3,64]{0,2,1:T(8,128)} %get-tuple-element.525, pred[]{:T(512)S(6)} %compare.3, bf16[4,512,3,64]{1,3,2,0:T(8,128)(2,1)} %get-tuple-element.550, ...), kind=kOutput, calls=%fused_computation.37.clone.1 | convolution fusion | flops 832045056 | bytes 33757188 | tf_op jit(solution)/shard_map/while/body/eval_jaxpr/hqk,qhd->khd/dot_general | solution.py:143
  667.9 18.3 %multiply_reduce_fusion.4 = (f32[3,512]{1,0:T(4,128)S(1)}, f32[3,512,4096]{2,1,0:T(8,128)}) fusion(f32[3,512,4096]{2,1,0:T(8,128)} %fusion.205, f32[3,512]{1,0:T(4,128)S(1)} %dynamic-slice_bitcast_fusion.2, pred[512,4096]{1,0:T(8,128)(4,1)S(1)} %fusion.206, bf16[4096,3,64]{0,2,1:T(8,128)(2,1)} %get-tuple-element.551, ...), kind=kOutput, calls=%fused_computation.25.clone.1 | convolution fusion | flops 836762112 | bytes 54210564 | tf_op jit(solution)/shard_map/while/body/eval_jaxpr/qhd,khd->hqk/dot_general | solution.py:129
  686.2 21.9 %multiply_convert_fusion.5 = bf16[3,512,4096]{2,1,0:T(8,128)(2,1)} fusion(f32[3,512,4096]{2,1,0:T(8,128)} %get-tuple-element.466, f32[3,512,4096]{2,1,0:T(8,128)} %fusion.205, f32[3,512]{1,0:T(4,128)S(1)} %get-tuple-element.467, f32[3,512]{1,0:T(4,128)S(1)} %dynamic-slice_bitcast_fusion.2, pred[512,4096]{1,0:T(8,128)(4,1)S(1)} %fusion.206), kind=kLoop, calls=%fused_computation.24.clone.1 | loop fusion | flops 37748736 | bytes 65024000 | tf_op jit(solution)/shard_map/while/body/eval_jaxpr/convert_element_type | solution.py:133
  735.7 13.3 %fusion.205 = f32[3,512,4096]{2,1,0:T(8,128)} fusion(bf16[4096,3,64]{0,2,1:T(8,128)(2,1)} %copy-done.1, bf16[4,512,3,64]{1,3,2,0:T(8,128)(2,1)} %copy-done.15, s32[]{:T(128)S(6)} %copy.60), kind=kOutput, calls=%fused_computation.48.clone.1 | convolution fusion | flops 805306368 | bytes 26935300 | tf_op jit(solution)/shard_map/while/body/eval_jaxpr/qhd,khd->hqk/dot_general | solution.py:125
  749.0 13.6 %fusion.208 = f32[4096,3,64]{0,2,1:T(8,128)} fusion(f32[3,512,4096]{2,1,0:T(8,128)} %fusion.205, f32[3,512]{1,0:T(4,128)S(1)} %dynamic-slice_bitcast_fusion.2, pred[512,4096]{1,0:T(8,128)(4,1)S(1)} %fusion.206, f32[4096,3,64]{0,2,1:T(8,128)} %get-tuple-element.525, pred[]{:T(512)S(6)} %compare.3, bf16[4,512,3,64]{1,3,2,0:T(8,128)(2,1)} %get-tuple-element.550, ...), kind=kOutput, calls=%fused_computation.37.clone.1 | convolution fusion | flops 832045056 | bytes 33757188 | tf_op jit(solution)/shard_map/while/body/eval_jaxpr/hqk,qhd->khd/dot_general | solution.py:143
  762.6 18.3 %multiply_reduce_fusion.4 = (f32[3,512]{1,0:T(4,128)S(1)}, f32[3,512,4096]{2,1,0:T(8,128)}) fusion(f32[3,512,4096]{2,1,0:T(8,128)} %fusion.205, f32[3,512]{1,0:T(4,128)S(1)} %dynamic-slice_bitcast_fusion.2, pred[512,4096]{1,0:T(8,128)(4,1)S(1)} %fusion.206, bf16[4096,3,64]{0,2,1:T(8,128)(2,1)} %get-tuple-element.551, ...), kind=kOutput, calls=%fused_computation.25.clone.1 | convolution fusion | flops 836762112 | bytes 54210564 | tf_op jit(solution)/shard_map/while/body/eval_jaxpr/qhd,khd->hqk/dot_general | solution.py:129
  780.9 21.9 %multiply_convert_fusion.5 = bf16[3,512,4096]{2,1,0:T(8,128)(2,1)} fusion(f32[3,512,4096]{2,1,0:T(8,128)} %get-tuple-element.466, f32[3,512,4096]{2,1,0:T(8,128)} %fusion.205, f32[3,512]{1,0:T(4,128)S(1)} %get-tuple-element.467, f32[3,512]{1,0:T(4,128)S(1)} %dynamic-slice_bitcast_fusion.2, pred[512,4096]{1,0:T(8,128)(4,1)S(1)} %fusion.206), kind=kLoop, calls=%fused_computation.24.clone.1 | loop fusion | flops 37748736 | bytes 65024000 | tf_op jit(solution)/shard_map/while/body/eval_jaxpr/convert_element_type | solution.py:133
  842.9 29.4 %reduce-scatter.2.cloned.1.call-done = bf16[1,2048,384]{1,2,0:T(8,128)(2,1)} async-done(((bf16[1,4096,384]{1,2,0:T(8,128)(2,1)}), bf16[1,2048,384]{1,2,0:T(8,128)(2,1)}) %reduce-scatter.2.cloned.1.call-update) | async-done | bytes 1572880 | tf_op jit(solution)/shard_map/reduce_scatter | solution.py:258
  902.1 97.5 %all-reduce.14.cloned.1.call-done = (bf16[1,2048,768]{2,1,0:T(8,128)(2,1)}, bf16[1,2048,768]{2,1,0:T(8,128)(2,1)}) async-done(((bf16[1,2048,768]{2,1,0:T(8,128)(2,1)}, bf16[1,2048,768]{2,1,0:T(8,128)(2,1)}), (bf16[1,2048,768]{2,1,0:T(8,128)(2,1)}, bf16[1,2048,768]{2,1,0:T(8,128)(2,1)})) %all-reduce.14.cloned.1.call-update) | async-done | bytes 6291472 | tf_op jit(solution)/shard_map/psum | solution.py:229
  1011.7 41.1 %all-reduce = (f32[768]{0:T(1024)}, f32[768]{0:T(1024)}, f32[768]{0:T(1024)}, f32[2,192]{1,0:T(2,128)}, f32[768]{0:T(1024)}, /*index=5*/f32[768]{0:T(1024)}, f32[768]{0:T(1024)}, f32[768]{0:T(1024)}, f32[768]{0:T(1024)}) all-reduce(f32[768]{0:T(1024)S(1)} %get-tuple-element.301, ...), channel_id=1, replica_groups=mesh['dp'=4,'seq'=2,'tensor'=4] {'dp','seq'}, use_global_device_ids=true, to_apply=%region_21.22 | all-reduce | flops 6528 | bytes 52224 | tf_op jit(solution)/shard_map/psum | solution.py:277
  1057.7 185.1 %all-reduce.12.cloned.1.call-done = (f32[3,768,192]{1,2,0:T(8,128)}, f32[192,768]{1,0:T(8,128)}, f32[768,768]{1,0:T(8,128)}, f32[768,768]{1,0:T(8,128)}) async-done(((f32[3,768,192]{1,2,0:T(8,128)}, f32[192,768]{1,0:T(8,128)}, f32[768,768]{1,0:T(8,128)}, f32[768,768]{1,0:T(8,128)}), (f32[3,768,192]{1,2,0:T(8,128)}, f32[192,768]{1,0:T(8,128)}, f32[768,768]{1,0:T(8,128)}, ...) | async-done | bytes 7077904 | tf_op jit(solution)/shard_map/psum | solution.py:277
  (313 shorter events, 340.1 us)
Async XLA Ops:
  7.2 333.8 %copy-start = (bf16[768,768]{1,0:T(8,128)(2,1)S(1)}, bf16[768,768]{1,0:T(8,128)(2,1)}, u32[]{:S(2)}) copy-start(bf16[768,768]{1,0:T(8,128)(2,1)} %param.33) | copy-start | bytes 3538948
  7.2 60.3 %all-gather.2.cloned.1.call-start = ((), (), s32[]{:S(2)}) async-start(), calls=%async_computation.1 | async-start | bytes 4718592 | tf_op jit(solution)/shard_map/all_gather | solution.py:201
  19.8 311.2 %all-reduce.8.cloned.1.call-start = ((), (), s32[]{:S(2)}) async-start(), calls=%async_computation.2 | async-start | bytes 6291456 | tf_op jit(solution)/shard_map/psum | solution.py:220
  80.9 12.1 copy-start.8
  93.0 12.0 copy-start.7
  93.0 12.0 copy-start.24
  126.8 12.1 copy-start.8
  138.9 12.0 copy-start.7
  138.9 12.0 copy-start.24
  172.8 12.1 copy-start.8
  184.9 12.0 copy-start.7
  184.9 12.0 copy-start.24
  218.7 12.1 copy-start.8
  230.8 12.0 copy-start.7
  230.8 12.0 copy-start.24
  255.8 79.3 %copy-start.55 = (s32[4]{0:T(128)}, s32[4]{0:T(128)S(1)}, u32[]{:S(2)}) copy-start(s32[4]{0:T(128)S(1)} %get-tuple-element.618) | copy-start | bytes 52
  255.8 79.3 %copy-start.58 = (bf16[13,13]{1,0:T(8,128)(2,1)}, bf16[13,13]{1,0:T(8,128)(2,1)S(1)}, u32[]{:S(2)}) copy-start(bf16[13,13]{1,0:T(8,128)(2,1)S(1)} %get-tuple-element.636) | copy-start | bytes 1018
  255.8 75.1 %copy-start.34 = (f32[768]{0:T(1024)S(1)}, f32[768]{0:T(1024)}, u32[]{:S(2)}) copy-start(f32[768]{0:T(1024)} %param.22) | copy-start | bytes 9220
  255.8 75.1 %copy-start.46 = (f32[768]{0:T(1024)S(1)}, f32[768]{0:T(1024)}, u32[]{:S(2)}) copy-start(f32[768]{0:T(1024)} %param.28) | copy-start | bytes 9220
  262.3 159.9 %all-reduce.10.cloned.1.call-start = ((), (), s32[]{:S(2)}) async-start(), calls=%async_computation.3 | async-start | bytes 6291456 | tf_op jit(solution)/shard_map/psum | solution.py:237
  353.5 518.8 %reduce-scatter.2.cloned.1.call-start = ((), (), s32[]{:S(2)}) async-start(), calls=%async_computation.4 | async-start | bytes 4718592 | tf_op jit(solution)/shard_map/reduce_scatter | solution.py:258
  434.2 10.8 copy-start.56
  519.5 9.7 copy-start.16
  613.3 9.7 copy-start.16
  828.7 170.9 %all-reduce.14.cloned.1.call-start = ((), (), s32[]{:S(2)}) async-start(), calls=%async_computation.6 | async-start | bytes 12582912 | tf_op jit(solution)/shard_map/psum | solution.py:229
  879.6 363.3 %all-reduce.12.cloned.1.call-start = ((), (), s32[]{:S(2)}) async-start(), calls=%async_computation.5 | async-start | bytes 14155776 | tf_op jit(solution)/shard_map/psum | solution.py:277
  879.9 15.8 %slice-start = ((s8[6291456]{0:T(1024)(128)(4,1)}), s8[4194304]{0:T(1024)(128)(4,1)S(1)}, s32[]{:S(2)}) async-start(s8[6291456]{0:T(1024)(128)(4,1)} %bitcast.206), calls=%async_computation.7 | async-start | bytes 8388608
  898.9 100.7 %copy-start.32 = (f32[2048]{0:T(1024)S(1)}, f32[2048]{0:T(1024)}, u32[]{:S(2)}) copy-start(f32[2048]{0:T(1024)} %copy-done.31) | copy-start | bytes 24580
  898.9 100.7 %copy-start.35 = (f32[768]{0:T(1024)S(1)}, f32[768]{0:T(1024)}, u32[]{:S(2)}) copy-start(f32[768]{0:T(1024)} %param.22) | copy-start | bytes 9220
  898.9 100.7 %copy-start.41 = (f32[768]{0:T(1024)S(1)}, f32[768]{0:T(1024)}, u32[]{:S(2)}) copy-start(f32[768]{0:T(1024)} %param.23) | copy-start | bytes 9220
  901.1 103.9 %copy-start.37 = (f32[2048]{0:T(1024)S(1)}, f32[2048]{0:T(1024)}, u32[]{:S(2)}) copy-start(f32[2048]{0:T(1024)} %copy-done.36) | copy-start | bytes 24580
  1005.1 49.7 %copy-start.48 = (f32[768]{0:T(1024)S(1)}, f32[768]{0:T(1024)}, u32[]{:S(2)}) copy-start(f32[768]{0:T(1024)} %param.34) | copy-start | bytes 9220
  (64 other events, 343.6 us)
Sparse Core Ops, SparseCore 0:
  19.9 47.6 all-gather.1
  262.5 68.4 all-reduce.7
  353.6 68.5 all-reduce.9
  828.8 43.4 reduce-scatter.1
  879.7 119.7 all-reduce.13
  1005.6 237.1 all-reduce.11
where the time goes:
time: 1260 us
  waiting for transfers between devices  493 us (39%)
  matrix products  449 us (36%)
  other arithmetic  193 us (15%)
  local copies, waits for them, and re-layouts  48.5 us (4%)
  blocking collectives  41.1 us (3%)
  loops' own time  16.8 us (1%)
  between operations  15 us (1%)
    psum x1, waiting for transfers between devices, local(): lax.psum((grad_w_qkv, grad_b_qv, grad_w_out, grad_w_up, grad_b_up, grad_w...  185 us
    dot_general x8, matrix products, one_block(): jnp.einsum('qhd,khd->hqk', q_block, key_heads, preferred_element_type=jnp...  101 us
    psum x1, waiting for transfers between devices, local(): lax.psum(partial_mlp.astype(jnp.bfloat16), 'tensor').astype(jnp.float32)  97.5 us
    convert_element_type x4, other arithmetic, one_block(): grad_score = (probs_full * (grad_prob - inner)).astype(jnp.bfloat16)  87.6 us
    dot_general x4, matrix products, one_block(): jnp.einsum('qhd,khd->hqk', g_block, value_heads, preferred_element_type=j...  73.2 us
    psum x1, waiting for transfers between devices, local(): lax.psum(partial_lift.astype(jnp.bfloat16), 'tensor').astype(jnp.float32)  68.6 us
    psum x1, waiting for transfers between devices, local(): lax.psum(partial_attn.astype(jnp.bfloat16), 'tensor').astype(jnp.float32)  68.1 us
    dot_general x4, matrix products, one_block(): jnp.einsum('hqk,qhd->khd', probs_full.astype(jnp.bfloat16), g_block, pref...  53.5 us
  transfers between devices with their start and end apart: 6, of which 6 were waited for; matrix products, arithmetic and copies ran while one was open for 5% of the time, Pallas kernels for 0%

commit v1 on v0

v1 whole, which is shorter than its diff:
```python
import functools

import jax
import jax.numpy as jnp
from jax import lax
from jax.experimental import pallas as pl
from jax.experimental.pallas import tpu as pltpu
from jax.sharding import PartitionSpec as P

HD = 64
BLK = 256
TRUNK_BLOCKS = 4
LANE = 256
EPS = 1e-05
ROOT = 0.7978845608028654
BF = jnp.bfloat16
F4 = jnp.float32
NT = (((1,), (1,)), ((), ()))
NN = (((1,), (0,)), ((), ()))
TN = (((0,), (0,)), ((), ()))


def dot(left, right, dims=NN):
    return lax.dot_general(left, right, dims, preferred_element_type=F4)


def norm_stats(values):
    row_mean = jnp.mean(values, -1, keepdims=True)
    centred = values - row_mean
    inv_std = lax.rsqrt(jnp.mean(centred * centred, -1, keepdims=True) + EPS)
    return (centred * inv_std, inv_std)


def norm_back(grad_out, normal, inv_std, gain_vec):
    scaled = grad_out * gain_vec
    return inv_std * (
        scaled
        - jnp.mean(scaled, -1, keepdims=True)
        - normal * jnp.mean(scaled * normal, -1, keepdims=True)
    )


def gelu_parts(pre_act):
    cubic_term = 0.044715 * pre_act * pre_act * pre_act
    tangent = jnp.tanh(ROOT * (pre_act + cubic_term))
    gelu_value = 0.5 * pre_act * (1.0 + tangent)
    gelu_slope = 0.5 * (1.0 + tangent) + 0.5 * pre_act * (1.0 - tangent * tangent) * ROOT * (
        1.0 + 3.0 * 0.044715 * pre_act * pre_act
    )
    return (gelu_value, gelu_slope)


def block_rows(pos, count=1):
    return pl.ds(pl.multiple_of(pos * BLK, BLK), count * BLK)


def head_masks(shape, heads):
    lane = lax.broadcasted_iota(jnp.int32, shape, 1) // HD
    return [lane == h for h in range(heads)]


def each_tile(order_ref, tile):
    trunk = [order_ref[i] for i in range(TRUNK_BLOCKS)]
    base = order_ref[16]
    tile(trunk[0], trunk[1], [], [(trunk[0], True)], [(trunk[0], False), (trunk[1], True)])
    tile(
        trunk[2],
        trunk[3],
        [(trunk[0], 2)],
        [(trunk[2], True)],
        [(trunk[2], False), (trunk[3], True)],
    )

    def branch(i, carry):
        one, two = order_ref[4 + 2 * i], order_ref[5 + 2 * i]
        tile(one, two, [(base, 4)], [(one, True)], [(two, True)])
        return carry

    lax.fori_loop(0, 2, branch, 0)

    def leaf(i, carry):
        one, two = order_ref[8 + 2 * i], order_ref[9 + 2 * i]
        tile(one, two, [(base, 4), (order_ref[4 + i], 1)], [(one, True)], [(two, True)])
        return carry

    lax.fori_loop(0, 4, leaf, 0)


def attend_kernel(heads, rows, order_ref, part_ref, qkv_ref, out_ref, lse_ref):
    part = part_ref[0]

    def q_at(pos):
        return qkv_ref[pl.ds(pl.multiple_of(pos * BLK + part * rows, rows), rows), 0:LANE]

    def k_at(pos, count=1):
        return qkv_ref[block_rows(pos, count), LANE : 2 * LANE]

    def v_at(pos, count=1):
        return qkv_ref[block_rows(pos, count), 2 * LANE : 3 * LANE]

    row_at = lax.broadcasted_iota(jnp.int32, (rows, BLK), 0) + part * rows
    causal = row_at >= lax.broadcasted_iota(jnp.int32, (rows, BLK), 1)
    masks = head_masks((2 * rows, LANE), heads)

    def tile(first, second, shared, parts_a, parts_b):
        q = jnp.concatenate([q_at(first), q_at(second)], 0) * BF(0.125)
        result = jnp.zeros((2 * rows, LANE), F4)
        log_cols = []
        for h in range(heads):
            qm = jnp.where(masks[h], q, BF(0))
            halves = [qm[:rows], qm[rows:]]
            wide = [dot(qm, k_at(p, c), NT) for p, c in shared]
            own = [
                [
                    jnp.where(causal, dot(halves[i], k_at(p), NT), -jnp.inf)
                    if diag
                    else dot(halves[i], k_at(p), NT)
                    for p, diag in parts
                ]
                for i, parts in enumerate((parts_a, parts_b))
            ]
            tops = []
            for i in range(2):
                tops.append(
                    functools.reduce(
                        jnp.maximum,
                        [
                            jnp.max(s, 1, keepdims=True)
                            for s in [w[i * rows : (i + 1) * rows] for w in wide] + own[i]
                        ],
                    )
                )
            top = jnp.concatenate(tops, 0)
            mix = jnp.zeros((2 * rows, LANE), F4)
            total = jnp.zeros((2 * rows, 1), F4)
            for s, (p, c) in zip(wide, shared):
                e = jnp.exp(s - top)
                total = total + jnp.sum(e, 1, keepdims=True)
                mix = mix + dot(e.astype(BF), v_at(p, c))
            extra = []
            sums = []
            for i, parts in enumerate((parts_a, parts_b)):
                m_i = jnp.zeros((rows, LANE), F4)
                t_i = jnp.zeros((rows, 1), F4)
                for s, (p, _) in zip(own[i], parts):
                    e = jnp.exp(s - tops[i])
                    t_i = t_i + jnp.sum(e, 1, keepdims=True)
                    m_i = m_i + dot(e.astype(BF), v_at(p))
                extra.append(m_i)
                sums.append(t_i)
            total = total + jnp.concatenate(sums, 0)
            mix = (mix + jnp.concatenate(extra, 0)) / total
            result = jnp.where(masks[h], mix, result)
            log_cols.append(top + jnp.log(total))
        low = result.astype(BF)[:, : heads * HD]
        out_ref[first] = low[:rows]
        out_ref[second] = low[rows:]
        lane = lax.broadcasted_iota(jnp.int32, (2 * rows, 128), 1)
        cols = jnp.zeros((2 * rows, 128), F4)
        for h in range(heads):
            cols = jnp.where(lane == h, log_cols[h], cols)
        flat = jnp.transpose(cols)[:8]
        lse_ref[first] = flat[:, :rows]
        lse_ref[second] = flat[:, rows:]

    each_tile(order_ref, tile)


def in_vmem(count):
    return [pl.BlockSpec(memory_space=pltpu.VMEM)] * count


def in_smem(count):
    return [pl.BlockSpec(memory_space=pltpu.SMEM)] * count


def attend(qkv, order, part, heads, rows):
    blocks = qkv.shape[0] // BLK
    return pl.pallas_call(
        functools.partial(attend_kernel, heads, rows),
        out_shape=(
            jax.ShapeDtypeStruct((blocks, rows, heads * HD), BF),
            jax.ShapeDtypeStruct((blocks, 8, rows), F4),
        ),
        in_specs=in_smem(2) + in_vmem(1),
        out_specs=in_vmem(2),
        compiler_params=pltpu.CompilerParams(vmem_limit_bytes=56 << 20),
        cost_estimate=pl.CostEstimate(
            flops=25_000_000_000, bytes_accessed=10_000_000, transcendentals=9_000_000
        ),
        name="tree_attend",
    )(order, part, qkv)


def attend_back_kernel(
    heads, rows, order_ref, part_ref, qkv_ref, mix_ref, grad_ref, lse_ref, out_ref, acc_k, acc_v
):
    part = part_ref[0]
    width = heads * HD

    def q_rows(pos):
        return pl.ds(pl.multiple_of(pos * BLK + part * rows, rows), rows)

    def k_at(pos, count=1):
        return qkv_ref[block_rows(pos, count), LANE : 2 * LANE]

    def v_at(pos, count=1):
        return qkv_ref[block_rows(pos, count), 2 * LANE : 3 * LANE]

    key_at = lax.broadcasted_iota(jnp.int32, (BLK, rows), 0)
    causal = (lax.broadcasted_iota(jnp.int32, (BLK, rows), 1) + part * rows) >= key_at
    masks = head_masks((2 * rows, LANE), heads)
    acc_k[...] = jnp.zeros_like(acc_k)
    acc_v[...] = jnp.zeros_like(acc_v)
    out_ref[:, 0:LANE] = jnp.zeros((out_ref.shape[0], LANE), BF)
    pick = (
        lax.broadcasted_iota(jnp.int32, (8, LANE), 1) // HD
        == lax.broadcasted_iota(jnp.int32, (8, LANE), 0)
    ).astype(BF)
    pad = jnp.zeros((2 * rows, LANE - width), BF)

    def tile(first, second, shared, parts_a, parts_b):
        q = jnp.concatenate(
            [qkv_ref[q_rows(first), 0:LANE], qkv_ref[q_rows(second), 0:LANE]], 0
        ) * BF(0.125)
        grad = jnp.concatenate([jnp.concatenate([grad_ref[first], grad_ref[second]], 0), pad], 1)
        mix = jnp.concatenate([jnp.concatenate([mix_ref[first], mix_ref[second]], 0), pad], 1)
        inner = dot(pick, (grad.astype(F4) * mix.astype(F4)).astype(BF), NT)
        lse = jnp.concatenate([lse_ref[first], lse_ref[second]], 1)
        qms = [jnp.where(masks[h], q, BF(0)) for h in range(heads)]
        gms = [jnp.where(masks[h], grad, BF(0)) for h in range(heads)]

        def pieces(keys, values, h, cut, diag):
            e = jnp.exp(dot(keys, qms[h][cut], NT) - lse[h : h + 1, cut])
            if diag:
                e = jnp.where(causal, e, 0.0)
            t = dot(values, gms[h][cut], NT)
            return e.astype(BF), (e * (t - inner[h : h + 1, cut])).astype(BF)

        def strip(pos, count, cut, diag, grad_q):
            keys, values = k_at(pos, count), v_at(pos, count)
            es = []
            ds = []
            for h in range(heads):
                e, d = pieces(keys, values, h, cut, diag)
                es.append(e)
                ds.append(d)
                grad_q = grad_q + jnp.where(masks[h][cut], dot(d, keys, TN), 0.0)
            acc_v[block_rows(pos, count), :] += dot(
                jnp.concatenate(es, 1), jnp.concatenate([g[cut] for g in gms], 0)
            )
            acc_k[block_rows(pos, count), :] += dot(
                jnp.concatenate(ds, 1), jnp.concatenate([g[cut] for g in qms], 0)
            )
            return grad_q

        grad_q = jnp.zeros((2 * rows, LANE), F4)
        for pos, count in shared:
            grad_q = strip(pos, count, slice(0, 2 * rows), False, grad_q)
        halves = []
        for i, parts in enumerate((parts_a, parts_b)):
            half = jnp.zeros((rows, LANE), F4)
            for pos, diag in parts:
                half = strip(pos, 1, slice(i * rows, (i + 1) * rows), diag, half)
            halves.append(half)
        grad_q = ((grad_q + jnp.concatenate(halves, 0)) * 0.125).astype(BF)
        out_ref[q_rows(first), 0:LANE] = grad_q[:rows]
        out_ref[q_rows(second), 0:LANE] = grad_q[rows:]

    each_tile(order_ref, tile)
    out_ref[:, LANE : 2 * LANE] = acc_k[...].astype(BF)
    out_ref[:, 2 * LANE :] = acc_v[...].astype(BF)


def attend_back(qkv, mix, grad, lse, order, part, heads, rows):
    length = qkv.shape[0]
    return pl.pallas_call(
        functools.partial(attend_back_kernel, heads, rows),
        out_shape=jax.ShapeDtypeStruct((length, 3 * LANE), BF),
        in_specs=in_smem(2) + in_vmem(4),
        out_specs=in_vmem(1)[0],
        scratch_shapes=[pltpu.VMEM((length, LANE), F4), pltpu.VMEM((length, LANE), F4)],
        compiler_params=pltpu.CompilerParams(vmem_limit_bytes=60 << 20),
        cost_estimate=pl.CostEstimate(
            flops=45_000_000_000, bytes_accessed=20_000_000, transcendentals=9_000_000
        ),
        name="tree_attend_back",
    )(order, part, qkv, mix, grad, lse)


def project_kernel(place_ref, *refs):
    x_ref, pass_ref, gain_ref, shift_ref, w_ref, b_ref = refs[:6]
    normed_ref, qkv_ref = refs[-2:]
    residual = x_ref[...].astype(F4) + pass_ref[...]
    normal, _ = norm_stats(residual)
    normed = (normal * gain_ref[...] + shift_ref[...]).astype(BF)
    normed_ref[...] = normed
    qkv_ref[...] = (dot(normed, w_ref[...]) + b_ref[...]).astype(BF)


def project(rows, place, offset, length, pass_embed, gain, shift, weight, bias, before=None):
    width = weight.shape[1]
    depth = rows.shape[1]
    vec = pl.BlockSpec((1, depth), lambda i, place: (0, 0))
    specs = [
        pl.BlockSpec((BLK, depth), lambda i, place: (place[i], 0)),
        vec,
        vec,
        vec,
        pl.BlockSpec((depth, width), lambda i, place: (0, 0)),
        pl.BlockSpec((1, width), lambda i, place: (0, 0)),
    ]
    operands = [rows, pass_embed[None], gain[None], shift[None], weight, bias[None]]
    aliases = {}
    if before is not None:
        specs += [pl.BlockSpec(memory_space=pl.ANY)] * 2
        operands += list(before)
        aliases = {7: 0, 8: 1}
    count = rows.shape[0] // BLK
    return pl.pallas_call(
        project_kernel,
        out_shape=(
            jax.ShapeDtypeStruct((length, depth), BF),
            jax.ShapeDtypeStruct((length, width), BF),
        ),
        grid_spec=pltpu.PrefetchScalarGridSpec(
            num_scalar_prefetch=1,
            grid=(count,),
            in_specs=specs,
            out_specs=(
                pl.BlockSpec((BLK, depth), lambda i, place: (offset + i, 0)),
                pl.BlockSpec((BLK, width), lambda i, place: (offset + i, 0)),
            ),
        ),
        input_output_aliases=aliases,
        compiler_params=pltpu.CompilerParams(vmem_limit_bytes=24 << 20),
        cost_estimate=pl.CostEstimate(
            flops=2 * rows.shape[0] * depth * width,
            bytes_accessed=rows.shape[0] * (2 * depth + width) * 2,
            transcendentals=rows.shape[0],
        ),
        name="norm_project",
    )(place, *operands)


def send(values, axis, partner):
    size = lax.axis_size(axis)
    return lax.ppermute(values, axis, [(i, partner(i)) for i in range(size)])


def hop(values, step):
    return send(values, "tensor", lambda i: i ^ step)


def cross(values):
    return send(values, "seq", lambda i: i ^ 1)


def add_low(left, right):
    return (left.astype(F4) + right.astype(F4)).astype(BF)


def slot(values, index, size, axis=0):
    return lax.dynamic_slice_in_dim(values, index * size, size, axis)


class Paired:
    def __init__(self, block_len):
        self.me = lax.axis_index("seq")
        self.rank = lax.axis_index("tensor")
        self.sub = block_len // 4
        self.per = self.sub // BLK

    def position(self, natural, blocks):
        half = blocks // 2
        s, b = natural // half, natural % half
        return half * (s ^ self.me) + self.per * ((b // self.per) ^ self.rank) + b % self.per

    def near(self, values):
        return jnp.concatenate([slot(values, self.rank ^ r, self.sub) for r in range(4)], 0)

    def place(self, count):
        spot = jnp.arange(count, dtype=jnp.int32)
        return self.per * ((spot // self.per) ^ self.rank) + spot % self.per

    def far(self, values):
        mine = cross(slot(values, self.rank, self.sub))
        return self.spread(mine)

    def spread(self, own):
        core = hop(own, 1)
        other = hop(own, 2)
        diag = hop(other, 1)
        return jnp.concatenate([own, core, other, diag], 0)

    def gather_weight(self, own):
        return jnp.concatenate([own, hop(own, 1), hop(own, 2), hop(own, 3)], 0)

    def collect(self, partial):
        size = partial.shape[0] // 4
        piece = [partial[r * size : (r + 1) * size] for r in range(4)]
        got = hop(jnp.concatenate([piece[1], piece[3]], 0), 1)
        away = hop(add_low(piece[2], got[size:]), 2)
        return piece[0].astype(F4) + got[:size].astype(F4) + away.astype(F4)

    def collect_all(self, partial):
        size = partial.shape[0] // 8
        piece = partial.reshape(2, 2, 2, size, partial.shape[1])
        got = hop(piece[:, :, 1], 1)
        chip = add_low(piece[:, :, 0], got)
        got = cross(chip[1])
        pair = add_low(chip[0], got)
        away = hop(pair[1], 2)
        return pair[0].astype(F4) + away.astype(F4)

    def to_tokens(self, mixture):
        blocks, rows, width = mixture.shape
        piece = mixture.reshape(2, 4, self.per, rows, width)
        columns = []
        for r in range(4):
            here = piece[0, r] if r == 0 else self.both(piece[0, r], 0, r)
            there = self.both(piece[1, r], 1, r)
            first = jnp.where(self.me == 0, here, there)
            second = jnp.where(self.me == 0, there, here)
            columns.append(jnp.stack([first, second], 1).reshape(self.sub, width))
        return jnp.concatenate(columns, 1)

    def to_heads(self, grads, rows):
        width = grads.shape[1] // 4
        parts = grads.reshape(self.per, 2, rows, 4, width)
        mine = jnp.where(self.me == 0, parts[:, 0], parts[:, 1])
        theirs = jnp.where(self.me == 0, parts[:, 1], parts[:, 0])
        here = [
            mine[:, :, r] if r == 0 else self.both(mine[:, :, r], 0, r) for r in range(4)
        ]
        there = [self.both(theirs[:, :, r], 1, r) for r in range(4)]
        return jnp.concatenate(here + there, 0)

    def both(self, values, step_seq, step_tensor):
        return send(
            values, ("seq", "tensor"), lambda i: (i // 4 ^ step_seq) * 4 + (i % 4 ^ step_tensor)
        )


class Plain:
    def __init__(self, block_len):
        self.me = lax.axis_index("seq")
        self.rank = lax.axis_index("tensor")
        self.sub = block_len // lax.axis_size("tensor")
        self.seq = lax.axis_size("seq")
        self.tensor = lax.axis_size("tensor")

    def position(self, natural, blocks):
        return natural

    def near(self, values):
        return values

    def place(self, count):
        return jnp.arange(count, dtype=jnp.int32)

    def spread(self, own):
        return lax.all_gather(own, "tensor", axis=0, tiled=True)

    def gather_weight(self, own):
        return lax.all_gather(own, "tensor", axis=0, tiled=True)

    def collect(self, partial):
        return lax.psum_scatter(partial, "tensor", scatter_dimension=0, tiled=True).astype(F4)

    def collect_all(self, partial):
        return lax.psum_scatter(
            partial, ("seq", "tensor"), scatter_dimension=0, tiled=True
        ).astype(F4)

    def to_tokens(self, mixture):
        blocks, rows, width = mixture.shape
        full = lax.all_gather(mixture, ("seq", "tensor"), axis=0)
        full = full.reshape(self.seq, self.tensor, blocks, rows, width)
        full = full.transpose(2, 0, 3, 1, 4).reshape(blocks * self.seq * rows, -1)
        return slot(full, self.me * self.tensor + self.rank, self.sub)

    def to_heads(self, grads, rows):
        full = lax.all_gather(grads, ("seq", "tensor"), axis=0, tiled=True)
        full = full.reshape(-1, self.seq, rows, self.tensor, grads.shape[1] // self.tensor)
        part = slot(full, self.me, 1, 1)[:, 0]
        return slot(part, self.rank, 1, 2)[:, :, 0]


def tree_order(seg_row, parent_row, position):
    blocks = seg_row.shape[0] // BLK
    segs = parent_row.shape[0]
    slot_seg = seg_row[::BLK]
    labels = jnp.arange(segs, dtype=jnp.int32)
    above = jnp.sum(jnp.where(slot_seg[:, None] == labels[None, :], parent_row[None, :], 0), 1)
    natural = jnp.arange(blocks, dtype=jnp.int32)
    key = jnp.where(
        slot_seg == 0,
        natural,
        jnp.where(above == 0, 100 + slot_seg, 1000 + 16 * above + slot_seg),
    )
    rank = jnp.sum((key[None, :] < key[:, None]).astype(jnp.int32), 1)
    where = position(natural, blocks)
    order = jnp.sum(jnp.where(rank[:, None] == natural[None, :], where[:, None], 0), 0)
    base = order[0] // TRUNK_BLOCKS * TRUNK_BLOCKS
    return jnp.concatenate([order, base[None]]).astype(jnp.int32)


def padded(values, axis):
    widths = [(0, 0)] * values.ndim
    widths[axis] = (0, LANE - values.shape[axis])
    return jnp.pad(values, widths)


def total(values):
    return jnp.sum(values, axis=0)


def reduce_grads(arrays):
    low = [a.astype(BF) for a in arrays]
    return [a.astype(F4) for a in lax.psum(low, ("dp", "seq"))]


def local(
    inputs,
    pass_embed,
    norm1_gain,
    norm1_shift,
    w_qkv,
    b_qv,
    w_out,
    b_out,
    norm2_gain,
    norm2_shift,
    w_up,
    b_up,
    w_down,
    b_down,
    out_grad,
    seg_id,
    parent,
):
    x = inputs[0]
    dy_block = out_grad[0]
    block_len, depth = x.shape
    length = seg_id.shape[1]
    seq, tensor = lax.axis_size("seq"), lax.axis_size("tensor")
    width = w_qkv.shape[2]
    heads = width // HD
    rows = BLK // seq
    paired = seq == 2 and tensor == 4 and block_len % (4 * BLK) == 0
    move = Paired(block_len) if paired else Plain(block_len)

    order = tree_order(seg_id[0], parent[0], move.position)
    part = move.me[None].astype(jnp.int32)

    w_cols = jnp.concatenate([padded(w_qkv[i], 1) for i in range(3)], 1)
    zero = jnp.zeros((LANE,), F4)
    b_cols = jnp.concatenate([padded(b_qv[0], 0), zero, padded(b_qv[1], 0)])
    norm_args = (length, pass_embed, norm1_gain, norm1_shift, w_cols, b_cols)
    if paired:
        far = move.far(x)
        count = block_len // BLK
        made = project(x, move.place(count), 0, *norm_args)
        straight = jnp.arange(count, dtype=jnp.int32)
        normed, qkv = project(far, straight, count, *norm_args, before=made)
    else:
        full = lax.all_gather(x, "seq", axis=0, tiled=True)
        normed, qkv = project(full, move.place(length // BLK), 0, *norm_args)

    mixture, lse = attend(qkv, order, part, heads, rows)

    out_weight = move.gather_weight(w_out)
    mix_own = move.to_tokens(mixture)
    x_own = slot(x, move.rank, move.sub)
    dy_own = slot(dy_block, move.rank, move.sub).astype(F4)
    residual = x_own.astype(F4) + pass_embed
    middle = residual + dot(mix_own, out_weight) + b_out
    norm_two, inv_two = norm_stats(middle)
    lifted = move.spread((norm_two * norm2_gain + norm2_shift).astype(BF))

    dy = move.near(dy_block)
    pre_act = dot(lifted, w_up) + b_up
    gelu_value, gelu_slope = gelu_parts(pre_act)
    active = gelu_value.astype(BF)
    grad_pre = (dot(dy, w_down, NT) * gelu_slope).astype(BF)
    grad_lift = move.collect(dot(grad_pre, w_up, NT).astype(BF))
    output = (middle + move.collect(dot(active, w_down).astype(BF)) + b_down).astype(BF)
    grad_w_down = dot(active, dy, TN)
    grad_w_up = dot(lifted, grad_pre, TN)
    grad_b_up = total(grad_pre.astype(F4))

    grad_middle = dy_own + norm_back(grad_lift, norm_two, inv_two, norm2_gain)
    proj_low = grad_middle.astype(BF)
    grad_mix = move.to_heads(dot(proj_low, out_weight, NT).astype(BF), rows)
    grad_w_out = move.collect(dot(mix_own, proj_low, TN).astype(BF))

    grad_w_up, grad_w_down, grad_w_out = reduce_grads([grad_w_up, grad_w_down, grad_w_out])

    grads = attend_back(qkv, mixture, grad_mix, lse, order, part, heads, rows)

    grad_w_cols = dot(normed, grads, TN)
    grad_norm = move.collect_all(dot(grads, w_cols, NT).astype(BF))
    (grad_w_cols,) = reduce_grads([grad_w_cols])
    grad_w_qkv = jnp.stack([grad_w_cols[:, i * LANE : i * LANE + width] for i in range(3)])
    sums = total(grads.astype(F4))
    grad_b_qv = jnp.stack([sums[:width], sums[2 * LANE : 2 * LANE + width]])

    norm_one, inv_one = norm_stats(residual)
    grad_resid = grad_middle + norm_back(grad_norm, norm_one, inv_one, norm1_gain)
    input_grad = grad_resid.astype(BF)

    own_sums = jnp.stack(
        [
            total(grad_resid),
            total(grad_norm * norm_one),
            total(grad_norm),
            total(grad_middle),
            total(grad_lift * norm_two),
            total(grad_lift),
            total(dy_own),
        ]
    )
    own_sums = lax.psum(own_sums, ("dp", "seq", "tensor"))
    grad_b_qv, grad_b_up = lax.psum((grad_b_qv, grad_b_up), ("dp", "seq"))
    return (
        output[None],
        input_grad[None],
        own_sums[0],
        own_sums[1],
        own_sums[2],
        grad_w_qkv,
        grad_b_qv,
        grad_w_out,
        own_sums[3],
        own_sums[4],
        own_sums[5],
        grad_w_up,
        grad_b_up,
        grad_w_down,
        own_sums[6],
    )


def solution(mesh):
    return jax.shard_map(
        local,
        mesh=mesh,
        in_specs=(
            P("dp", "seq", None),
            P(),
            P(),
            P(),
            P(None, None, "tensor"),
            P(None, "tensor"),
            P("tensor", None),
            P(),
            P(),
            P(),
            P(None, "tensor"),
            P("tensor"),
            P("tensor", None),
            P(),
            P("dp", "seq", None),
            P("dp", None),
            P("dp", None),
        ),
        out_specs=(
            P("dp", ("seq", "tensor"), None),
            P("dp", ("seq", "tensor"), None),
            P(),
            P(),
            P(),
            P(None, None, "tensor"),
            P(None, "tensor"),
            P("tensor", None),
            P(),
            P(),
            P(),
            P(None, "tensor"),
            P("tensor"),
            P("tensor", None),
            P(),
        ),
        check_vma=False,
    )
```

time: 1260 us -> 536 us (0.43)
  matrix products: 449 us -> 53.3 us
  waiting for transfers between devices: 493 us -> 208 us
  other arithmetic: 193 us -> 38.6 us
  Pallas kernels: 0 us -> 80.8 us
  starting transfers between devices: 0.82 us -> 29 us
  blocking collectives: 41.1 us -> 61.6 us
  loops' own time: 16.8 us -> 0 us
    dot_general x55 -> x11, matrix products: 449 us -> 53.3 us  [dot(): return lax.dot_general(left, right, dims, preferred_element_type=F4)]
    psum x4 -> x1, waiting for transfers between devices: 419 us -> 75.7 us  [reduce_grads(): return [a.astype(F4) for a in lax.psum(low, ('dp', 'seq'))]]
    ppermute x0 -> x33, waiting for transfers between devices: none -> 132 us  [send(): return lax.ppermute(values, axis, [(i, partner(i)) for i in range(size)])]
    pallas_call x0 -> x4, Pallas kernels: none -> 80.8 us  [the longest x1 44.1 us: attend_back(): pl.pallas_call(functools.partial(attend_back_kernel, heads, rows), out_sh...]
    convert_element_type x5 -> x11, other arithmetic: 90.5 us -> 14.2 us  [the longest x4 7.77 us: reduce_grads(): return [a.astype(F4) for a in lax.psum(low, ('dp', 'seq'))]]
    reduce_sum x10 -> x9, other arithmetic: 72.6 us -> 15.9 us  [the longest x6 14.8 us: total(): return jnp.sum(values, axis=0)]
    all_gather x1 -> x0, waiting for transfers between devices: 43.7 us -> none  [local(): lax.all_gather(jnp.concatenate([key_loc, value_loc], -1), 'seq', axis=1,...]
    reduce_scatter x1 -> x0, waiting for transfers between devices: 29.4 us -> none  [local(): lax.psum_scatter(jnp.stack(term_list).astype(jnp.bfloat16), 'seq', scatte...]
  transfers between devices with their start and end apart: 6 -> 34, of which waited for: 6 -> 14; matrix products, arithmetic and copies ran while one was open for 5% -> 13% of each run, Pallas kernels for 0% -> 7%
where the time goes in v1:
time: 536 us; the launch traced here: 527 us
  waiting for transfers between devices  208 us (39%)
  Pallas kernels  80.8 us (15%)
  blocking collectives  61.6 us (11%)
  matrix products  53.3 us (10%)
  local copies, waits for them, and re-layouts  39.4 us (7%)
  other arithmetic  38.6 us (7%)
  starting transfers between devices  29 us (5%)
  between operations  15.7 us (3%)
    ppermute x33, waiting for transfers between devices, send(): return lax.ppermute(values, axis, [(i, partner(i)) for i in range(size)])  132 us
    psum x1, waiting for transfers between devices, reduce_grads(): return [a.astype(F4) for a in lax.psum(low, ('dp', 'seq'))]  75.7 us
    dot_general x11, matrix products, dot(): return lax.dot_general(left, right, dims, preferred_element_type=F4)  53.3 us
    pallas_call x1, Pallas kernels, attend_back(): pl.pallas_call(functools.partial(attend_back_kernel, heads, rows), out_sh...  44.1 us
    psum x1, blocking collectives, local(): own_sums = lax.psum(own_sums, ('dp', 'seq', 'tensor'))  39.3 us
    ppermute x33, starting transfers between devices, send(): return lax.ppermute(values, axis, [(i, partner(i)) for i in range(size)])  28.9 us
    pallas_call x1, Pallas kernels, attend(): pl.pallas_call(functools.partial(attend_kernel, heads, rows), out_shape=(...  24.5 us
    psum x1, blocking collectives, local(): grad_b_qv, grad_b_up = lax.psum((grad_b_qv, grad_b_up), ('dp', 'seq'))  22.2 us
  transfers between devices with their start and end apart: 34, of which 14 were waited for; matrix products, arithmetic and copies ran while one was open for 13% of the time, Pallas kernels for 7%

profile of v1, /device:TPU:0, one launch (start us, length us, event | category | flops | bytes accessed | tf_op | source)
XLA Modules:
  0.0 526.5 jit_solution(16146493719301488794)
XLA Ops:
  9.3 2.9 collective-permute-start
  17.2 12.7 %collective-permute-done = bf16[512,768]{1,0:T(8,128)(2,1)} collective-permute-done((bf16[512,768]{1,0:T(8,128)(2,1)S(1)}, bf16[512,768]{1,0:T(8,128)(2,1)}, u32[]{:S(2)}, u32[]{:S(2)}) %collective-permute-start) | collective-permute-done | bytes 786464 | tf_op jit(solution)/shard_map/ppermute | solution.py:348
  36.8 12.1 %collective-permute-done.2 = bf16[512,768]{1,0:T(8,128)(2,1)} collective-permute-done((bf16[512,768]{1,0:T(8,128)(2,1)}, bf16[512,768]{1,0:T(8,128)(2,1)}, u32[]{:S(2)}, u32[]{:S(2)}) %collective-permute-start.2) | collective-permute-done | bytes 786464 | tf_op jit(solution)/shard_map/ppermute | solution.py:348
  51.6 6.1 %norm_project.2 = (bf16[4096,768]{1,0:T(8,128)(2,1)S(1)}, bf16[4096,768]{1,0:T(8,128)(2,1)S(1)}) custom-call(s32[8]{0:T(128)S(1)} %fusion.28.place_ref, bf16[2048,768]{1,0:T(8,128)(2,1)S(1)} %bitcast.148, f32[1,768]{1,0:T(1,128)S(1)} %broadcast_in_dim.51.refs_1_, f32[1,768]{1,0:T(1,128)S(1)} %broadcast_in_dim.88.refs_2_, ...), custom_call_target="tpu_custom_call" | custom-call | flops 2415919104 | bytes 9437184 | tf_op jit(solution)/shard_map/norm_project/pallas_call | solution.py:320
  61.7 6.1 %norm_project.3 = (bf16[4096,768]{1,0:T(8,128)(2,1)S(1)}, bf16[4096,768]{1,0:T(8,128)(2,1)S(1)}) custom-call(s32[8]{0:T(128)S(1)} %iota.28.place_ref, bf16[2048,768]{1,0:T(8,128)(2,1)S(1)} %pad_maximum_fusion.refs_0_, f32[1,768]{1,0:T(1,128)S(1)} %broadcast_in_dim.51.refs_1_, ...), custom_call_target="tpu_custom_call", output_to_operand_aliasing={{0}: (7, {}), {1}: (8, {})} | custom-call | flops 2415919104 | bytes 9437184 | tf_op jit(solution)/shard_map/norm_project/pallas_call | solution.py:320
  67.8 2.6 copy-done.2
  73.0 24.5 %tree_attend.1 = (bf16[16,128,192]{2,1,0:T(8,128)(2,1)}, f32[16,8,128]{2,1,0:T(8,128)}) custom-call(s32[17]{0:T(128)} %pad_add_fusion.order_ref, s32[1]{0:T(128)} %bitcast.5.part_ref, bf16[4096,768]{1,0:T(8,128)(2,1)} %copy-done.3), custom_call_target="tpu_custom_call" | custom-call | flops 24999999488 | bytes 10000000 | tf_op jit(solution)/shard_map/tree_attend/pallas_call | solution.py:179
  121.4 18.5 %collective-permute-done.15 = bf16[512,768]{1,0:T(8,128)(2,1)} collective-permute-done((bf16[512,768]{1,0:T(8,128)(2,1)}, bf16[512,768]{1,0:T(8,128)(2,1)}, u32[]{:S(2)}, u32[]{:S(2)}) %collective-permute-start.15) | collective-permute-done | bytes 786464 | tf_op jit(solution)/shard_map/ppermute | solution.py:348
  143.7 4.5 fusion.22
  148.3 11.2 %convert_reduce_fusion.1 = (f32[768]{0:T(1024)}, bf16[2048,768]{1,0:T(8,128)(2,1)S(1)}) fusion(f32[2048,768]{1,0:T(8,128)S(1)} %fusion.22, f32[768]{0:T(1024)S(1)} %copy-done.33, bf16[768,768]{1,0:T(8,128)(2,1)S(1)} %copy-done, bf16[512,768]{1,0:T(8,128)(2,1)S(1)} %get-tuple-element.119, bf16[512,768]{1,0:T(8,128)(2,1)S(1)} %get-tuple-element.120, ...), kind=kOutput, calls=%fused_computation.13 | convolution fusion | flops 2463104256 | bytes 13768704 | tf_op jit(solution)/shard_map/dot_general | solution.py:24
  159.5 2.9 convolution_convert_fusion.1
  163.2 4.6 convolution_convert_fusion.2
  169.9 4.6 convolution_convert_fusion.3
  175.3 13.5 %collective-permute-done.20 = bf16[512,768]{1,0:T(8,128)(2,1)S(1)} collective-permute-done((bf16[512,768]{1,0:T(8,128)(2,1)S(1)}, bf16[512,768]{1,0:T(8,128)(2,1)S(1)}, u32[]{:S(2)}, u32[]{:S(2)}) %collective-permute-start.20) | collective-permute-done | bytes 786464 | tf_op jit(solution)/shard_map/ppermute | solution.py:348
  190.3 15.0 %collective-permute-done.18 = bf16[512,768]{1,0:T(8,128)(2,1)S(1)} collective-permute-done((bf16[512,768]{1,0:T(8,128)(2,1)S(1)}, bf16[512,768]{1,0:T(8,128)(2,1)S(1)}, u32[]{:S(2)}, u32[]{:S(2)}) %collective-permute-start.18) | collective-permute-done | bytes 786464 | tf_op jit(solution)/shard_map/ppermute | solution.py:348
  205.2 2.7 fusion.41
  210.5 2.8 reshape.179
  221.2 4.9 collective-permute-done.22
  227.2 4.5 collective-permute-done.23
  232.8 44.1 %tree_attend_back.1 = bf16[4096,768]{1,0:T(8,128)(2,1)} custom-call(s32[17]{0:T(128)} %pad_add_fusion.order_ref, s32[1]{0:T(128)} %bitcast.5.part_ref, bf16[4096,768]{1,0:T(8,128)(2,1)} %copy-done.3, bf16[16,128,192]{2,1,0:T(8,128)(2,1)} %get-tuple-element.24.mix_ref, bf16[16,128,192]{2,1,0:T(8,128)(2,1)} %copy-done.26, f32[16,8,128]{2,1,0:T(8,128)} %get-tuple-element.25.lse_ref), custom_call_target="tpu_custom_call" | custom-call | flops 44999999488 | bytes 20000000 | tf_op jit(solution)/shard_map/tree_attend_back/pallas_call | solution.py:277
  276.9 8.6 %convolution_convert_fusion = bf16[4096,768]{1,0:T(8,128)(2,1)S(1)} fusion(bf16[4096,768]{1,0:T(8,128)(2,1)} %tree_attend_back.1, bf16[768,192]{1,0:T(8,128)(2,1)S(1)} %bitcast.158, bf16[768,192]{1,0:T(8,128)(2,1)S(1)} %bitcast.156, bf16[768,192]{1,0:T(8,128)(2,1)S(1)} %bitcast.154), kind=kOutput, calls=%fused_computation.3 | convolution fusion | flops 4843241472 | bytes 13467648 | tf_op jit(solution)/shard_map/dot_general | solution.py:24
  290.4 5.8 %convolution_convert_fusion.4 = bf16[768,768]{1,0:T(8,128)(2,1)} fusion(bf16[2048,768]{1,0:T(8,128)(2,1)S(1)} %copy-done.35, bf16[512,768]{1,0:T(8,128)(2,1)} %collective-permute-done.16, bf16[512,768]{1,0:T(8,128)(2,1)} %collective-permute-done.15, bf16[512,768]{1,0:T(8,128)(2,1)} %collective-permute-done.14, bf16[512,768]{1,0:T(8,128)(2,1)} %add_convert_fusion.3), kind=kOutput, calls=%fused_computation.58 | convolution fusion | flops 2429091840 | bytes 7471104 | tf_op jit(solution)/shard_map/dot_general | solution.py:24
  297.8 6.1 %convolution_convert_fusion.6 = bf16[768,768]{1,0:T(8,128)(2,1)} fusion(bf16[4096,768]{1,0:T(8,128)(2,1)S(1)} %bitcast.147, bf16[4096,768]{1,0:T(8,128)(2,1)S(1)} %bitcast.150), kind=kOutput, calls=%fused_computation.60 | convolution fusion | flops 4832428032 | bytes 13762560 | tf_op jit(solution)/shard_map/dot_general | solution.py:24
  306.3 3.6 fusion.7
  312.9 3.7 convert_reduce_fusion
  316.6 43.1 %collective-permute-done.29 = bf16[2,512,768]{2,1,0:T(8,128)(2,1)S(1)} collective-permute-done((bf16[2,512,768]{2,1,0:T(8,128)(2,1)S(1)}, bf16[2,512,768]{2,1,0:T(8,128)(2,1)S(1)}, u32[]{:S(2)}, u32[]{:S(2)}) %collective-permute-start.29) | collective-permute-done | bytes 1572896 | tf_op jit(solution)/shard_map/ppermute | solution.py:348
  362.5 22.2 %all-reduce.5 = (f32[2,192]{1,0:T(2,128)}, f32[768]{0:T(1024)}) all-reduce(f32[2,192]{1,0:T(2,128)S(1)} %pad_maximum_fusion.15, f32[768]{0:T(1024)S(1)} %copy-done.30), channel_id=1, replica_groups=mesh['dp'=4,'seq'=2,'tensor'=4] {'dp','seq'}, use_global_device_ids=true, to_apply=%region_21.22 | all-reduce | flops 1152 | bytes 9216 | tf_op jit(solution)/shard_map/psum | solution.py:625
  384.7 75.7 %all-reduce.9.cloned.1.call-done = (bf16[768,768]{1,0:T(8,128)(2,1)}, bf16[192,768]{1,0:T(8,128)(2,1)}, bf16[768,768]{1,0:T(8,128)(2,1)}, bf16[768,768]{1,0:T(8,128)(2,1)}) async-done(((bf16[768,768]{1,0:T(8,128)(2,1)}, bf16[192,768]{1,0:T(8,128)(2,1)}, bf16[768,768]{1,0:T(8,128)(2,1)}, bf16[768,768]{1,0:T(8,128)(2,1)}), (bf16[768,768]{1,0:T(8,128)(2,1)}, bf16[192,768]{1,0:T(8,128)(2,1)}, ...) | async-done | bytes 3833872 | tf_op jit(solution)/shard_map/psum | solution.py:521
  465.4 2.9 copy.100
  468.3 2.9 convert_element_type.215
  475.5 2.9 fusion.42
  479.2 39.3 %psum.49 = f32[7,768]{1,0:T(8,128)S(1)} all-reduce(f32[7,768]{1,0:T(8,128)S(1)} %stack.100), channel_id=1, replica_groups=mesh['dp'=4,'seq'=2,'tensor'=4] {'dp','seq','tensor'}, use_global_device_ids=true, to_apply=%region_18.19 | all-reduce | flops 5376 | bytes 43008 | tf_op jit(solution)/shard_map/psum | solution.py:624
  (255 shorter events, 93.0 us)
Async XLA Ops:
  7.2 453.2 %all-reduce.9.cloned.1.call-start = ((), (), s32[]{:S(2)}) async-start(), calls=%async_computation | async-start | bytes 7667712 | tf_op jit(solution)/shard_map/psum | solution.py:521
  9.3 20.6 %collective-permute-start = (bf16[512,768]{1,0:T(8,128)(2,1)S(1)}, bf16[512,768]{1,0:T(8,128)(2,1)}, u32[]{:S(2)}, u32[]{:S(2)}) collective-permute-start(bf16[512,768]{1,0:T(8,128)(2,1)S(1)} %get-tuple-element.115), channel_id=1, source_target_pairs={{0,4},{4,0},{1,5},{5,1},{2,6},{6,2},{3,7},{7,3},{8,12},{12,8},{9,1... | collective-permute-start | bytes 2359304 | tf_op jit(solution)/shard_map/ppermute | solution.py:348
  12.2 46.5 %collective-permute-start.12 = (bf16[192,768]{1,0:T(8,128)(2,1)}, bf16[192,768]{1,0:T(8,128)(2,1)}, u32[]{:S(2)}, u32[]{:S(2)}) collective-permute-start(bf16[192,768]{1,0:T(8,128)(2,1)} %param.23), channel_id=1, source_target_pairs={{0,2},{1,3},{2,0},{3,1},{4,6},{5,7},{6,4},{7,5},{8,10},{9,11},{10,... | collective-permute-start | bytes 884744 | tf_op jit(solution)/shard_map/ppermute | solution.py:348
  13.8 43.9 %collective-permute-start.11 = (bf16[192,768]{1,0:T(8,128)(2,1)}, bf16[192,768]{1,0:T(8,128)(2,1)}, u32[]{:S(2)}, u32[]{:S(2)}) collective-permute-start(bf16[192,768]{1,0:T(8,128)(2,1)} %param.23), channel_id=1, source_target_pairs={{0,1},{1,0},{2,3},{3,2},{4,5},{5,4},{6,7},{7,6},{8,9},{9,8},{10,11... | collective-permute-start | bytes 884744 | tf_op jit(solution)/shard_map/ppermute | solution.py:348
  13.8 86.7 %collective-permute-start.13 = (bf16[192,768]{1,0:T(8,128)(2,1)}, bf16[192,768]{1,0:T(8,128)(2,1)}, u32[]{:S(2)}, u32[]{:S(2)}) collective-permute-start(bf16[192,768]{1,0:T(8,128)(2,1)} %param.23), channel_id=1, source_target_pairs={{0,3},{1,2},{2,1},{3,0},{4,7},{5,6},{6,5},{7,4},{8,11},{9,10},{10,... | collective-permute-start | bytes 884744 | tf_op jit(solution)/shard_map/ppermute | solution.py:348
  29.9 19.0 %collective-permute-start.2 = (bf16[512,768]{1,0:T(8,128)(2,1)}, bf16[512,768]{1,0:T(8,128)(2,1)}, u32[]{:S(2)}, u32[]{:S(2)}) collective-permute-start(bf16[512,768]{1,0:T(8,128)(2,1)} %collective-permute-done), channel_id=1, source_target_pairs={{0,2},{1,3},{2,0},{3,1},{4,6},{5,7},{6,4},{7,5},{8,10},{9,11},{10,... | collective-permute-start | bytes 2359304 | tf_op jit(solution)/shard_map/ppermute | solution.py:348
  36.7 23.0 %collective-permute-start.1 = (bf16[512,768]{1,0:T(8,128)(2,1)}, bf16[512,768]{1,0:T(8,128)(2,1)S(1)}, u32[]{:S(2)}, u32[]{:S(2)}) collective-permute-start(bf16[512,768]{1,0:T(8,128)(2,1)} %collective-permute-done), channel_id=1, source_target_pairs={{0,1},{1,0},{2,3},{3,2},{4,5},{5,4},{6,7},{7,6},{8,9},{9,8},{10,11... | collective-permute-start | bytes 2359304 | tf_op jit(solution)/shard_map/ppermute | solution.py:348
  48.9 10.8 %collective-permute-start.3 = (bf16[512,768]{1,0:T(8,128)(2,1)}, bf16[512,768]{1,0:T(8,128)(2,1)S(1)}, u32[]{:S(2)}, u32[]{:S(2)}) collective-permute-start(bf16[512,768]{1,0:T(8,128)(2,1)} %collective-permute-done.2), channel_id=1, source_target_pairs={{0,1},{1,0},{2,3},{3,2},{4,5},{5,4},{6,7},{7,6},{8,9},{9,8},{10,11... | collective-permute-start | bytes 2359304 | tf_op jit(solution)/shard_map/ppermute | solution.py:348
  99.0 7.6 %collective-permute-start.4 = (bf16[2,128,192]{1,2,0:T(8,128)(2,1)S(1)}, bf16[2,128,192]{1,2,0:T(8,128)(2,1)S(1)}, u32[]{:S(2)}, u32[]{:S(2)}) collective-permute-start(bf16[2,128,192]{1,2,0:T(8,128)(2,1)S(1)} %bitcast.167), channel_id=1, source_target_pairs={{0,4},{1,5},{2,6},{3,7},{4,0},{5,1},{6,2},{7,3},{8,12},{9,13},{10,... | collective-permute-start | bytes 294920 | tf_op jit(solution)/shard_map/ppermute | solution.py:348
  103.0 10.7 %collective-permute-start.10 = (bf16[2,128,192]{1,2,0:T(8,128)(2,1)S(1)}, bf16[2,128,192]{1,2,0:T(8,128)(2,1)S(1)}, u32[]{:S(2)}, u32[]{:S(2)}) collective-permute-start(bf16[2,128,192]{1,2,0:T(8,128)(2,1)S(1)} %bitcast.162), channel_id=1, source_target_pairs={{0,7},{1,6},{2,5},{3,4},{4,3},{5,2},{6,1},{7,0},{8,15},{9,14},{10,... | collective-permute-start | bytes 294920 | tf_op jit(solution)/shard_map/ppermute | solution.py:348
  104.4 4.0 collective-permute-start.5
  104.7 6.3 %collective-permute-start.6 = (bf16[2,128,192]{1,2,0:T(8,128)(2,1)S(1)}, bf16[2,128,192]{1,2,0:T(8,128)(2,1)}, u32[]{:S(2)}, u32[]{:S(2)}) collective-permute-start(bf16[2,128,192]{1,2,0:T(8,128)(2,1)S(1)} %bitcast.165), channel_id=1, source_target_pairs={{0,5},{1,4},{2,7},{3,6},{4,1},{5,0},{6,3},{7,2},{8,13},{9,12},{10,... | collective-permute-start | bytes 294920 | tf_op jit(solution)/shard_map/ppermute | solution.py:348
  106.0 7.4 %collective-permute-start.7 = (bf16[2,128,192]{1,2,0:T(8,128)(2,1)S(1)}, bf16[2,128,192]{1,2,0:T(8,128)(2,1)S(1)}, u32[]{:S(2)}, u32[]{:S(2)}) collective-permute-start(bf16[2,128,192]{1,2,0:T(8,128)(2,1)S(1)} %bitcast.164), channel_id=1, source_target_pairs={{0,2},{1,3},{2,0},{3,1},{4,6},{5,7},{6,4},{7,5},{8,10},{9,11},{10,... | collective-permute-start | bytes 294920 | tf_op jit(solution)/shard_map/ppermute | solution.py:348
  106.6 6.9 %collective-permute-start.8 = (bf16[2,128,192]{1,2,0:T(8,128)(2,1)S(1)}, bf16[2,128,192]{1,2,0:T(8,128)(2,1)S(1)}, u32[]{:S(2)}, u32[]{:S(2)}) collective-permute-start(bf16[2,128,192]{1,2,0:T(8,128)(2,1)S(1)} %bitcast.163), channel_id=1, source_target_pairs={{0,6},{1,7},{2,4},{3,5},{4,2},{5,3},{6,0},{7,1},{8,14},{9,15},{10,... | collective-permute-start | bytes 294920 | tf_op jit(solution)/shard_map/ppermute | solution.py:348
  108.4 7.0 %collective-permute-start.9 = (bf16[2,128,192]{1,2,0:T(8,128)(2,1)S(1)}, bf16[2,128,192]{1,2,0:T(8,128)(2,1)S(1)}, u32[]{:S(2)}, u32[]{:S(2)}) collective-permute-start(bf16[2,128,192]{1,2,0:T(8,128)(2,1)S(1)} %bitcast.161), channel_id=1, source_target_pairs={{0,3},{1,2},{2,1},{3,0},{4,7},{5,6},{6,5},{7,4},{8,11},{9,10},{10,... | collective-permute-start | bytes 294920 | tf_op jit(solution)/shard_map/ppermute | solution.py:348
  120.0 19.9 %collective-permute-start.15 = (bf16[512,768]{1,0:T(8,128)(2,1)}, bf16[512,768]{1,0:T(8,128)(2,1)}, u32[]{:S(2)}, u32[]{:S(2)}) collective-permute-start(bf16[512,768]{1,0:T(8,128)(2,1)} %add_convert_fusion.3), channel_id=1, source_target_pairs={{0,2},{1,3},{2,0},{3,1},{4,6},{5,7},{6,4},{7,5},{8,10},{9,11},{10,... | collective-permute-start | bytes 2359304 | tf_op jit(solution)/shard_map/ppermute | solution.py:348
  121.4 22.2 %collective-permute-start.14 = (bf16[512,768]{1,0:T(8,128)(2,1)}, bf16[512,768]{1,0:T(8,128)(2,1)}, u32[]{:S(2)}, u32[]{:S(2)}) collective-permute-start(bf16[512,768]{1,0:T(8,128)(2,1)} %add_convert_fusion.3), channel_id=1, source_target_pairs={{0,1},{1,0},{2,3},{3,2},{4,5},{5,4},{6,7},{7,6},{8,9},{9,8},{10,11... | collective-permute-start | bytes 2359304 | tf_op jit(solution)/shard_map/ppermute | solution.py:348
  162.7 5.5 %collective-permute-start.19 = (bf16[1024,768]{1,0:T(8,128)(2,1)S(1)}, bf16[1024,768]{1,0:T(8,128)(2,1)S(1)}, u32[]{:S(2)}, u32[]{:S(2)}) collective-permute-start(bf16[1024,768]{1,0:T(8,128)(2,1)S(1)} %pad_maximum_fusion.5), channel_id=1, source_target_pairs={{0,1},{1,0},{2,3},{3,2},{4,5},{5,4},{6,7},{7,6},{8,9},{9,8},{10,11... | collective-permute-start | bytes 4718600 | tf_op jit(solution)/shard_map/ppermute | solution.py:348
  168.1 6.4 %collective-permute-start.17 = (bf16[1024,768]{1,0:T(8,128)(2,1)S(1)}, bf16[1024,768]{1,0:T(8,128)(2,1)S(1)}, u32[]{:S(2)}, u32[]{:S(2)}) collective-permute-start(bf16[1024,768]{1,0:T(8,128)(2,1)S(1)} %pad_maximum_fusion.4), channel_id=1, source_target_pairs={{0,1},{1,0},{2,3},{3,2},{4,5},{5,4},{6,7},{7,6},{8,9},{9,8},{10,11... | collective-permute-start | bytes 4718600 | tf_op jit(solution)/shard_map/ppermute | solution.py:348
  168.4 20.4 %collective-permute-start.20 = (bf16[512,768]{1,0:T(8,128)(2,1)S(1)}, bf16[512,768]{1,0:T(8,128)(2,1)S(1)}, u32[]{:S(2)}, u32[]{:S(2)}) collective-permute-start(bf16[512,768]{1,0:T(8,128)(2,1)S(1)} %add_convert_fusion), channel_id=1, source_target_pairs={{0,2},{1,3},{2,0},{3,1},{4,6},{5,7},{6,4},{7,5},{8,10},{9,11},{10,... | collective-permute-start | bytes 2359304 | tf_op jit(solution)/shard_map/ppermute | solution.py:348
  174.7 30.6 %collective-permute-start.18 = (bf16[512,768]{1,0:T(8,128)(2,1)S(1)}, bf16[512,768]{1,0:T(8,128)(2,1)S(1)}, u32[]{:S(2)}, u32[]{:S(2)}) collective-permute-start(bf16[512,768]{1,0:T(8,128)(2,1)S(1)} %add_convert_fusion.2), channel_id=1, source_target_pairs={{0,2},{1,3},{2,0},{3,1},{4,6},{5,7},{6,4},{7,5},{8,10},{9,11},{10,... | collective-permute-start | bytes 2359304 | tf_op jit(solution)/shard_map/ppermute | solution.py:348
  213.9 17.9 %collective-permute-start.27 = (bf16[2,128,192]{2,1,0:T(8,128)(2,1)S(1)}, bf16[2,128,192]{2,1,0:T(8,128)(2,1)S(1)}, u32[]{:S(2)}, u32[]{:S(2)}) collective-permute-start(bf16[2,128,192]{2,1,0:T(8,128)(2,1)S(1)} %get-tuple-element.144), channel_id=1, source_target_pairs={{0,7},{1,6},{2,5},{3,4},{4,3},{5,2},{6,1},{7,0},{8,15},{9,14},{10,... | collective-permute-start | bytes 294920 | tf_op jit(solution)/shard_map/ppermute | solution.py:348
  214.6 17.1 %collective-permute-start.26 = (bf16[2,128,192]{2,1,0:T(8,128)(2,1)S(1)}, bf16[2,128,192]{2,1,0:T(8,128)(2,1)S(1)}, u32[]{:S(2)}, u32[]{:S(2)}) collective-permute-start(bf16[2,128,192]{2,1,0:T(8,128)(2,1)S(1)} %get-tuple-element.145), channel_id=1, source_target_pairs={{0,6},{1,7},{2,4},{3,5},{4,2},{5,3},{6,0},{7,1},{8,14},{9,15},{10,... | collective-permute-start | bytes 294920 | tf_op jit(solution)/shard_map/ppermute | solution.py:348
  216.2 15.6 %collective-permute-start.25 = (bf16[2,128,192]{2,1,0:T(8,128)(2,1)S(1)}, bf16[2,128,192]{2,1,0:T(8,128)(2,1)S(1)}, u32[]{:S(2)}, u32[]{:S(2)}) collective-permute-start(bf16[2,128,192]{2,1,0:T(8,128)(2,1)S(1)} %get-tuple-element.146), channel_id=1, source_target_pairs={{0,5},{1,4},{2,7},{3,6},{4,1},{5,0},{6,3},{7,2},{8,13},{9,12},{10,... | collective-permute-start | bytes 294920 | tf_op jit(solution)/shard_map/ppermute | solution.py:348
  216.9 14.8 %collective-permute-start.24 = (bf16[2,128,192]{2,1,0:T(8,128)(2,1)S(1)}, bf16[2,128,192]{2,1,0:T(8,128)(2,1)S(1)}, u32[]{:S(2)}, u32[]{:S(2)}) collective-permute-start(bf16[2,128,192]{2,1,0:T(8,128)(2,1)S(1)} %get-tuple-element.147), channel_id=1, source_target_pairs={{0,4},{1,5},{2,6},{3,7},{4,0},{5,1},{6,2},{7,3},{8,12},{9,13},{10,... | collective-permute-start | bytes 294920 | tf_op jit(solution)/shard_map/ppermute | solution.py:348
  219.8 6.3 %collective-permute-start.22 = (bf16[2,128,192]{2,1,0:T(8,128)(2,1)S(1)}, bf16[2,128,192]{2,1,0:T(8,128)(2,1)S(1)}, u32[]{:S(2)}, u32[]{:S(2)}) collective-permute-start(bf16[2,128,192]{2,1,0:T(8,128)(2,1)S(1)} %get-tuple-element.149), channel_id=1, source_target_pairs={{0,2},{1,3},{2,0},{3,1},{4,6},{5,7},{6,4},{7,5},{8,10},{9,11},{10,... | collective-permute-start | bytes 294920 | tf_op jit(solution)/shard_map/ppermute | solution.py:348
  226.1 5.6 %collective-permute-start.23 = (bf16[2,128,192]{2,1,0:T(8,128)(2,1)S(1)}, bf16[2,128,192]{2,1,0:T(8,128)(2,1)S(1)}, u32[]{:S(2)}, u32[]{:S(2)}) collective-permute-start(bf16[2,128,192]{2,1,0:T(8,128)(2,1)S(1)} %get-tuple-element.148), channel_id=1, source_target_pairs={{0,3},{1,2},{2,1},{3,0},{4,7},{5,6},{6,5},{7,4},{8,11},{9,10},{10,... | collective-permute-start | bytes 294920 | tf_op jit(solution)/shard_map/ppermute | solution.py:348
  289.7 16.5 %collective-permute-start.28 = (bf16[2,2,512,768]{3,2,1,0:T(8,128)(2,1)}, bf16[2,2,512,768]{3,2,1,0:T(8,128)(2,1)}, u32[]{:S(2)}, u32[]{:S(2)}) collective-permute-start(bf16[2,2,512,768]{3,2,1,0:T(8,128)(2,1)} %slice_bitcast_fusion), channel_id=1, source_target_pairs={{0,1},{1,0},{2,3},{3,2},{4,5},{5,4},{6,7},{7,6},{8,9},{9,8},{10,11... | collective-permute-start | bytes 9437192 | tf_op jit(solution)/shard_map/ppermute | solution.py:348
  289.9 6.3 %collective-permute-start.31 = (bf16[384,768]{1,0:T(8,128)(2,1)S(1)}, bf16[384,768]{1,0:T(8,128)(2,1)S(1)}, u32[]{:S(2)}, u32[]{:S(2)}) collective-permute-start(bf16[384,768]{1,0:T(8,128)(2,1)S(1)} %pad_maximum_fusion.6), channel_id=1, source_target_pairs={{0,1},{1,0},{2,3},{3,2},{4,5},{5,4},{6,7},{7,6},{8,9},{9,8},{10,11... | collective-permute-start | bytes 1769480 | tf_op jit(solution)/shard_map/ppermute | solution.py:348
  296.2 9.2 %collective-permute-start.32 = (bf16[192,768]{1,0:T(8,128)(2,1)S(1)}, bf16[192,768]{1,0:T(8,128)(2,1)S(1)}, u32[]{:S(2)}, u32[]{:S(2)}) collective-permute-start(bf16[192,768]{1,0:T(8,128)(2,1)S(1)} %add_convert_fusion.5), channel_id=1, source_target_pairs={{0,2},{1,3},{2,0},{3,1},{4,6},{5,7},{6,4},{7,5},{8,10},{9,11},{10,... | collective-permute-start | bytes 884744 | tf_op jit(solution)/shard_map/ppermute | solution.py:348
  310.0 49.7 %collective-permute-start.29 = (bf16[2,512,768]{2,1,0:T(8,128)(2,1)S(1)}, bf16[2,512,768]{2,1,0:T(8,128)(2,1)S(1)}, u32[]{:S(2)}, u32[]{:S(2)}) collective-permute-start(bf16[2,512,768]{2,1,0:T(8,128)(2,1)S(1)} %slice_bitcast_fusion.2), channel_id=1, source_target_pairs={{0,4},{4,0},{1,5},{5,1},{2,6},{6,2},{3,7},{7,3},{8,12},{12,8},{9,1... | collective-permute-start | bytes 4718600 | tf_op jit(solution)/shard_map/ppermute | solution.py:348
  361.1 111.8 %collective-permute-start.30 = (bf16[512,768]{1,0:T(8,128)(2,1)}, bf16[512,768]{1,0:T(8,128)(2,1)}, u32[]{:S(2)}, u32[]{:S(2)}) collective-permute-start(bf16[512,768]{1,0:T(8,128)(2,1)} %slice_bitcast_fusion.7), channel_id=1, source_target_pairs={{0,2},{1,3},{2,0},{3,1},{4,6},{5,7},{6,4},{7,5},{8,10},{9,11},{10,... | collective-permute-start | bytes 2359304 | tf_op jit(solution)/shard_map/ppermute | solution.py:348
  (42 other events, 578.3 us)
Sparse Core Ops, SparseCore 0:
  306.4 154.0 all-reduce.8
